TPU v7x, 128 devices: a whole 4x4x4 slice. The times are simulated.
128 devices in a mesh: seg: 4 (over x), chan: 32 (over z, y, core).
Axes of the slice: x: 4, y: 4, z: 4, core: 2. Of those that a mesh axis runs over, the one named last changes fastest.
Arguments:
- strain_rate: bfloat16 [48, 1024, 4096], P('seg', None, 'chan'), may hold values from -6 to 6
- window_length: int32 [48], P('seg'), may hold values from 1024 to 4096, as said below
- source_channel: int32 [128], replicated, may hold values from 0 to 1023, as said below
Outputs:
- stacked: float32 [1024, 128, 512], P('chan', 'seg')
Inputs may be any that keep to these rules, and one draw needn't show every extreme that they name: `window_length`: window 0 is fully recorded and window 1 holds exactly 1024 recorded samples. `source_channel`: the virtual sources are distinct channels; channel 0 and the last channel are always among them.
All inputs are finite; a program needn't handle non-finite values.
Results may differ from a plain program's by a relative error of at most 0.0045.
Values may be sent and summed in bfloat16 or wider, within the bound.
A program may use at most 128 MiB of HBM per device.

v0:
```python
import math

import jax
import jax.numpy as jnp
from jax import lax
from jax.sharding import PartitionSpec as P

W = 4096
NF = 1152
FIRST_BIN = 16
SMOOTH = 64
MAXLAG = 256
LAGS = 512


def angles(first, second):
    product = jnp.mod(first[:, None] * second[None, :], W)
    return product.astype(jnp.float32) * (2.0 * math.pi / W)


def spectrum_of(signal):
    block_bins = 384
    samples = jnp.arange(W, dtype=jnp.int32)
    real_parts = []
    imag_parts = []
    for begin in range(0, NF, block_bins):
        freqs = FIRST_BIN + begin + jnp.arange(block_bins, dtype=jnp.int32)
        phase = angles(samples, freqs)
        table = jnp.concatenate([jnp.cos(phase), -jnp.sin(phase)], axis=1).astype(jnp.bfloat16)
        result = jnp.dot(signal, table, preferred_element_type=jnp.float32)
        real_parts.append(result[:, :block_bins])
        imag_parts.append(result[:, block_bins:])
    return (jnp.concatenate(real_parts, axis=1), jnp.concatenate(imag_parts, axis=1))


def transform(windows):
    count, channels, length = windows.shape
    spec_real, spec_imag = spectrum_of(windows.reshape(count * channels, length))
    offsets = jnp.arange(NF, dtype=jnp.int32)
    nearby = jnp.abs(offsets[:, None] - offsets[None, :]) <= SMOOTH
    counts = jnp.sum(nearby.astype(jnp.float32), axis=0)
    magnitude = jnp.sqrt(spec_real * spec_real + spec_imag * spec_imag).astype(jnp.bfloat16)
    smooth = (
        jnp.dot(magnitude, nearby.astype(jnp.bfloat16), preferred_element_type=jnp.float32) / counts
        + 1e-06
    )
    white_real = (spec_real / smooth).astype(jnp.bfloat16).reshape(count, channels, NF)
    white_imag = (spec_imag / smooth).astype(jnp.bfloat16).reshape(count, channels, NF)
    return (white_real, white_imag)


def on_device(strain_rate, window_length, source_channel):
    chan_index = lax.axis_index("chan")
    local_samples = strain_rate.shape[2]
    sample_index = chan_index * local_samples + jnp.arange(local_samples, dtype=jnp.int32)
    inside = sample_index[None, :] < window_length[:, None]
    masked = jnp.where(inside[:, None, :], strain_rate, jnp.zeros((), jnp.bfloat16))
    regrouped = lax.all_to_all(masked, "chan", split_axis=1, concat_axis=2, tiled=True)
    white_real, white_imag = transform(regrouped)
    segwin = white_real.shape[0]
    ch_local = white_real.shape[1]
    channel_ids = chan_index * ch_local + jnp.arange(ch_local, dtype=jnp.int32)
    selector = (source_channel[:, None] == channel_ids[None, :]).astype(jnp.bfloat16)
    picked_real = jnp.einsum(
        "sc,wck->wsk", selector, white_real, preferred_element_type=jnp.bfloat16
    )
    picked_imag = jnp.einsum(
        "sc,wck->wsk", selector, white_imag, preferred_element_type=jnp.bfloat16
    )
    source_real, source_imag = (
        lax.psum(picked_real, "chan").astype(jnp.float32),
        lax.psum(picked_imag, "chan").astype(jnp.float32),
    )
    source_real = source_real.astype(jnp.bfloat16)
    source_imag = source_imag.astype(jnp.bfloat16)
    freqs = FIRST_BIN + jnp.arange(NF, dtype=jnp.int32)
    shifts = jnp.arange(LAGS, dtype=jnp.int32) - MAXLAG
    phase = angles(freqs, shifts)
    lag_table = jnp.concatenate([jnp.cos(phase), -jnp.sin(phase)], axis=0).astype(jnp.bfloat16)
    block_size = math.gcd(ch_local, 8)
    block_count = ch_local // block_size
    sources_count = source_real.shape[1]

    def correlate(start):
        part_real = lax.dynamic_slice_in_dim(white_real, start, block_size, 1)
        part_imag = lax.dynamic_slice_in_dim(white_imag, start, block_size, 1)
        cross_real = jnp.einsum(
            "wck,wsk->csk", part_real, source_real, preferred_element_type=jnp.float32
        ) + jnp.einsum("wck,wsk->csk", part_imag, source_imag, preferred_element_type=jnp.float32)
        cross_imag = jnp.einsum(
            "wck,wsk->csk", part_imag, source_real, preferred_element_type=jnp.float32
        ) - jnp.einsum("wck,wsk->csk", part_real, source_imag, preferred_element_type=jnp.float32)
        joined = jnp.concatenate([cross_real, cross_imag], axis=-1).astype(jnp.bfloat16)
        joined = joined.reshape(block_size * sources_count, 2 * NF)
        product = jnp.dot(joined, lag_table, preferred_element_type=jnp.float32)
        return product.reshape(block_size, sources_count, LAGS)

    starts = jnp.arange(block_count, dtype=jnp.int32) * block_size
    lag_stack = lax.map(correlate, starts).reshape(ch_local, sources_count, LAGS)
    seg_count = lax.axis_size("seg")
    scale = 1.0 / math.sqrt(NF * segwin * seg_count)
    whole_sum = lax.psum(lag_stack, "seg")
    share_size = sources_count // seg_count
    summed = lax.dynamic_slice_in_dim(whole_sum, lax.axis_index("seg") * share_size, share_size, 1)
    return summed * scale


def solution(mesh):
    in_specs = (P("seg", None, "chan"), P("seg"), P())
    out_specs = P("chan", "seg", None)
    return jax.shard_map(
        on_device, mesh=mesh, in_specs=in_specs, out_specs=out_specs, check_vma=False
    )
```

profile of v0, /device:TPU:1, one launch (start us, length us, event | category | flops | bytes accessed | tf_op | source)
XLA Modules:
  0.0 621.6 jit_solution(11344855177507847700)
XLA Ops:
  7.3 5.7 copy_select_fusion
  13.0 9.6 %all-to-all-start = ((bf16[12,1024,128]{2,0,1:T(8,128)(2,1)}), bf16[12,1024,128]{2,0,1:T(8,128)(2,1)}, u32[]{:S(2)}, u32[]{:S(2)}) async-start(bf16[12,1024,128]{2,0,1:T(8,128)(2,1)} %copy_select_fusion), calls=%async_computation | async-start | bytes 8388608 | tf_op jit(solution)/shard_map/all_to_all | solution.py:58
  23.0 26.4 %cosine_convert_fusion.2 = (bf16[4096,384]{1,0:T(8,128)(2,1)S(1)}, bf16[4096,384]{1,0:T(8,128)(2,1)}) fusion(s32[384]{0:T(512)S(1)} %iota_add_fusion.4), kind=kLoop, calls=%fused_computation.50 | loop fusion | flops 26738688 | bytes 6292992 | tf_op jit(solution)/shard_map/convert.10
  49.4 26.9 %cosine_convert_fusion.1 = (bf16[4096,384]{1,0:T(8,128)(2,1)}, bf16[4096,384]{1,0:T(8,128)(2,1)}) fusion(s32[384]{0:T(512)S(1)} %iota_add_fusion.3), kind=kLoop, calls=%fused_computation.46 | loop fusion | flops 26738688 | bytes 6292992 | tf_op jit(solution)/shard_map/convert.8
  76.3 27.1 %cosine_convert_fusion = (bf16[4096,384]{1,0:T(8,128)(2,1)}, bf16[4096,384]{1,0:T(8,128)(2,1)}) fusion(s32[384]{0:T(512)S(1)} %iota_add_fusion.2), kind=kLoop, calls=%fused_computation.42 | loop fusion | flops 26738688 | bytes 6292992 | tf_op jit(solution)/shard_map/convert.6
  103.4 4.4 copy.18
  107.8 2.9 fusion.26
  110.9 2.9 fusion.18
  113.9 2.9 fusion.22
  117.0 1.8 divide_convert_fusion
  118.8 3.5 convolution_bitcast_fusion
  122.3 3.0 convolution_bitcast_fusion.1
  125.4 10.2 %cosine_convert_fusion.3 = (bf16[1152,512]{1,0:T(8,128)(2,1)S(1)}, bf16[1152,512]{1,0:T(8,128)(2,1)S(1)}) fusion(s32[512]{0:T(512)S(1)} %iota_add_fusion.1, s32[1152]{0:T(1024)S(1)} %iota_add_fusion), kind=kLoop, calls=%fused_computation.81 | loop fusion | flops 10027008 | bytes 2365952 | tf_op jit(solution)/shard_map/convert.4
  135.6 1.6 pad_maximum_fusion.1
  137.2 106.5 %all-reduce.6.cloned.1.call-done = (bf16[12,128,1152]{1,2,0:T(8,128)(2,1)}, bf16[12,128,1152]{1,2,0:T(8,128)(2,1)}) async-done(((bf16[12,128,1152]{1,2,0:T(8,128)(2,1)}, bf16[12,128,1152]{1,2,0:T(8,128)(2,1)}), (bf16[12,128,1152]{1,2,0:T(8,128)(2,1)}, bf16[12,128,1152]{1,2,0:T(8,128)(2,1)})) %all-reduce.6.cloned.1.call-update) | async-done | bytes 7077904 | tf_op jit(solution)/shard_map/psum | solution.py:71
  243.8 13.0 %copy.20 = bf16[12,128,1152]{1,0,2:T(8,128)(2,1)} copy(bf16[12,128,1152]{1,2,0:T(8,128)(2,1)} %get-tuple-element.96) | data formatting | bytes 7077888 | tf_op jit(solution)/shard_map/while | solution.py:99
  256.8 13.8 %copy.22 = bf16[12,128,1152]{1,0,2:T(8,128)(2,1)} copy(bf16[12,128,1152]{1,2,0:T(8,128)(2,1)S(1)} %copy-done.5) | data formatting | bytes 7077888 | tf_op jit(solution)/shard_map/while | solution.py:99
  270.6 181.0 %while.10 = (s32[]{:T(128)}, f32[4,8,128,512]{3,2,1,0:T(8,128)}, s32[4]{0:T(128)S(1)}, bf16[12,32,1152]{2,1,0:T(8,128)(2,1)S(1)}, bf16[12,128,1152]{1,0,2:T(8,12...) while((s32[]{:T(128)}, f32[4,8,128,512]{3,2,1,0:T(8,128)}, ...), condition=%wide.region_4.5_spmd, body=%wide.region_3.4_spmd.sunk | while | flops 2536243200 | bytes 97649544 | solution.py:99
  273.7 2.3 copy.48
  276.1 5.9 fusion.106
  281.9 2.8 copy.47
  284.7 5.9 fusion.107
  290.7 3.2 fusion.104
  295.5 16.5 %pad_maximum_fusion.5 = bf16[8,128,2304]{1,0,2:T(8,128)(2,1)S(1)} fusion(bf16[8,128,1152]{1,0,2:T(8,128)(2,1)S(1)} %fusion.105, bf16[8,128,1152]{1,0,2:T(8,128)(2,1)S(1)} %fusion.107), kind=kLoop, calls=%fused_computation.clone.1 | loop fusion | flops 2359296 | bytes 9437184 | tf_op jit(solution)/shard_map/while/body/eval_jaxpr/concatenate | solution.py:93
  312.0 4.0 bitcast_dynamic-update-slice_fusion.2
  318.9 2.3 copy.48
  321.3 5.9 fusion.106
  327.1 2.8 copy.47
  329.9 5.9 fusion.107
  335.9 3.2 fusion.104
  340.7 16.5 %pad_maximum_fusion.5 = bf16[8,128,2304]{1,0,2:T(8,128)(2,1)S(1)} fusion(bf16[8,128,1152]{1,0,2:T(8,128)(2,1)S(1)} %fusion.105, bf16[8,128,1152]{1,0,2:T(8,128)(2,1)S(1)} %fusion.107), kind=kLoop, calls=%fused_computation.clone.1 | loop fusion | flops 2359296 | bytes 9437184 | tf_op jit(solution)/shard_map/while/body/eval_jaxpr/concatenate | solution.py:93
  357.2 3.9 bitcast_dynamic-update-slice_fusion.2
  364.1 2.3 copy.48
  366.4 5.9 fusion.106
  372.3 2.8 copy.47
  375.1 5.9 fusion.107
  381.0 3.2 fusion.104
  385.9 16.5 %pad_maximum_fusion.5 = bf16[8,128,2304]{1,0,2:T(8,128)(2,1)S(1)} fusion(bf16[8,128,1152]{1,0,2:T(8,128)(2,1)S(1)} %fusion.105, bf16[8,128,1152]{1,0,2:T(8,128)(2,1)S(1)} %fusion.107), kind=kLoop, calls=%fused_computation.clone.1 | loop fusion | flops 2359296 | bytes 9437184 | tf_op jit(solution)/shard_map/while/body/eval_jaxpr/concatenate | solution.py:93
  402.4 4.0 bitcast_dynamic-update-slice_fusion.2
  409.3 2.3 copy.48
  411.6 5.9 fusion.106
  417.5 2.8 copy.47
  420.3 5.9 fusion.107
  426.2 3.2 fusion.104
  431.1 16.5 %pad_maximum_fusion.5 = bf16[8,128,2304]{1,0,2:T(8,128)(2,1)S(1)} fusion(bf16[8,128,1152]{1,0,2:T(8,128)(2,1)S(1)} %fusion.105, bf16[8,128,1152]{1,0,2:T(8,128)(2,1)S(1)} %fusion.107), kind=kLoop, calls=%fused_computation.clone.1 | loop fusion | flops 2359296 | bytes 9437184 | tf_op jit(solution)/shard_map/while/body/eval_jaxpr/concatenate | solution.py:93
  447.6 4.0 bitcast_dynamic-update-slice_fusion.2
  451.7 159.6 %all-reduce.4.cloned.1.call-done = f32[32,128,512]{2,1,0:T(8,128)} async-done(((f32[32,128,512]{2,1,0:T(8,128)}), f32[32,128,512]{2,1,0:T(8,128)}) %all-reduce.4.cloned.1.call-update) | async-done | bytes 8388624 | tf_op jit(solution)/shard_map/psum | solution.py:102
  611.3 3.3 dynamic-slice_multiply_fusion
  (112 shorter events, 11.5 us)
Async XLA Ops:
  13.0 90.4 %all-to-all-start = ((bf16[12,1024,128]{2,0,1:T(8,128)(2,1)}), bf16[12,1024,128]{2,0,1:T(8,128)(2,1)}, u32[]{:S(2)}, u32[]{:S(2)}) async-start(bf16[12,1024,128]{2,0,1:T(8,128)(2,1)} %copy_select_fusion), calls=%async_computation | async-start | bytes 8388608 | tf_op jit(solution)/shard_map/all_to_all | solution.py:58
  22.7 221.1 %all-reduce.6.cloned.1.call-start = ((), (), s32[]{:S(2)}) async-start(), calls=%async_computation.2 | async-start | bytes 14155776 | tf_op jit(solution)/shard_map/psum | solution.py:71
  103.4 4.4 copy-start.9
  103.4 4.4 copy-start.10
  107.8 3.0 copy-start.6
  110.9 3.0 copy-start.7
  110.9 3.0 copy-start.8
  117.0 1.8 copy-start.12
  125.3 486.0 %all-reduce.4.cloned.1.call-start = ((), (), s32[]{:S(2)}) async-start(), calls=%async_computation.1 | async-start | bytes 16777216 | tf_op jit(solution)/shard_map/psum | solution.py:102
  243.8 13.0 %copy-start.5 = (bf16[12,128,1152]{1,2,0:T(8,128)(2,1)S(1)}, bf16[12,128,1152]{1,2,0:T(8,128)(2,1)}, u32[]{:S(2)}) copy-start(bf16[12,128,1152]{1,2,0:T(8,128)(2,1)} %get-tuple-element.97) | copy-start | bytes 10616836
  270.8 2.9 copy-start.1
  270.8 2.9 copy-start.3
  281.9 11.9 %slice-start = ((s8[4718592]{0:T(1024)(128)(4,1)}), s8[524288]{0:T(1024)(128)(4,1)S(1)}, s32[]{:S(2)}) async-start(s8[4718592]{0:T(1024)(128)(4,1)} %bitcast.71), calls=%async_computation.3 | async-start | bytes 1048576 | tf_op jit(solution)/shard_map/while
  284.7 6.0 copy-start
  284.7 9.2 %slice-start.1 = ((s8[4718592]{0:T(1024)(128)(4,1)}), s8[4194304]{0:T(1024)(128)(4,1)S(1)}, s32[]{:S(2)}) async-start(s8[4718592]{0:T(1024)(128)(4,1)} %bitcast.71), calls=%async_computation.4 | async-start | bytes 8388608 | tf_op jit(solution)/shard_map/while
  295.5 16.5 %copy-start.11 = (bf16[2304,512]{1,0:T(8,128)(2,1)S(1)}, bf16[2304,512]{1,0:T(8,128)(2,1)}, u32[]{:S(2)}) copy-start(bf16[2304,512]{1,0:T(8,128)(2,1)} %get-tuple-element.200) | copy-start | bytes 7077892 | tf_op jit(solution)/shard_map/while
  312.0 4.0 copy-start.2
  312.0 4.0 copy-start.4
  316.0 2.9 copy-start.1
  316.0 2.9 copy-start.3
  327.1 11.9 %slice-start = ((s8[4718592]{0:T(1024)(128)(4,1)}), s8[524288]{0:T(1024)(128)(4,1)S(1)}, s32[]{:S(2)}) async-start(s8[4718592]{0:T(1024)(128)(4,1)} %bitcast.71), calls=%async_computation.3 | async-start | bytes 1048576 | tf_op jit(solution)/shard_map/while
  329.9 6.0 copy-start
  329.9 9.2 %slice-start.1 = ((s8[4718592]{0:T(1024)(128)(4,1)}), s8[4194304]{0:T(1024)(128)(4,1)S(1)}, s32[]{:S(2)}) async-start(s8[4718592]{0:T(1024)(128)(4,1)} %bitcast.71), calls=%async_computation.4 | async-start | bytes 8388608 | tf_op jit(solution)/shard_map/while
  340.7 16.5 %copy-start.11 = (bf16[2304,512]{1,0:T(8,128)(2,1)S(1)}, bf16[2304,512]{1,0:T(8,128)(2,1)}, u32[]{:S(2)}) copy-start(bf16[2304,512]{1,0:T(8,128)(2,1)} %get-tuple-element.200) | copy-start | bytes 7077892 | tf_op jit(solution)/shard_map/while
  357.2 4.0 copy-start.2
  357.2 4.0 copy-start.4
  361.2 2.9 copy-start.1
  361.2 2.9 copy-start.3
  372.3 11.9 %slice-start = ((s8[4718592]{0:T(1024)(128)(4,1)}), s8[524288]{0:T(1024)(128)(4,1)S(1)}, s32[]{:S(2)}) async-start(s8[4718592]{0:T(1024)(128)(4,1)} %bitcast.71), calls=%async_computation.3 | async-start | bytes 1048576 | tf_op jit(solution)/shard_map/while
  375.0 6.0 copy-start
  375.0 9.2 %slice-start.1 = ((s8[4718592]{0:T(1024)(128)(4,1)}), s8[4194304]{0:T(1024)(128)(4,1)S(1)}, s32[]{:S(2)}) async-start(s8[4718592]{0:T(1024)(128)(4,1)} %bitcast.71), calls=%async_computation.4 | async-start | bytes 8388608 | tf_op jit(solution)/shard_map/while
  385.9 16.5 %copy-start.11 = (bf16[2304,512]{1,0:T(8,128)(2,1)S(1)}, bf16[2304,512]{1,0:T(8,128)(2,1)}, u32[]{:S(2)}) copy-start(bf16[2304,512]{1,0:T(8,128)(2,1)} %get-tuple-element.200) | copy-start | bytes 7077892 | tf_op jit(solution)/shard_map/while
  402.3 4.0 copy-start.2
  402.4 4.0 copy-start.4
  406.4 2.9 copy-start.1
  406.4 2.9 copy-start.3
  417.5 11.9 %slice-start = ((s8[4718592]{0:T(1024)(128)(4,1)}), s8[524288]{0:T(1024)(128)(4,1)S(1)}, s32[]{:S(2)}) async-start(s8[4718592]{0:T(1024)(128)(4,1)} %bitcast.71), calls=%async_computation.3 | async-start | bytes 1048576 | tf_op jit(solution)/shard_map/while
  420.3 6.0 copy-start
  420.3 9.2 %slice-start.1 = ((s8[4718592]{0:T(1024)(128)(4,1)}), s8[4194304]{0:T(1024)(128)(4,1)S(1)}, s32[]{:S(2)}) async-start(s8[4718592]{0:T(1024)(128)(4,1)} %bitcast.71), calls=%async_computation.4 | async-start | bytes 8388608 | tf_op jit(solution)/shard_map/while
  431.1 16.5 %copy-start.11 = (bf16[2304,512]{1,0:T(8,128)(2,1)S(1)}, bf16[2304,512]{1,0:T(8,128)(2,1)}, u32[]{:S(2)}) copy-start(bf16[2304,512]{1,0:T(8,128)(2,1)} %get-tuple-element.200) | copy-start | bytes 7077892 | tf_op jit(solution)/shard_map/while
  447.6 4.1 copy-start.2
  447.6 4.1 copy-start.4
Sparse Core Ops, SparseCore 0:
  125.5 118.2 all-reduce.5
  451.8 159.4 all-reduce.3
where the time goes:
time: 627 us; the launch traced here: 622 us
  waiting for transfers between devices  266 us (42%)
  other arithmetic  168 us (27%)
  matrix products  99.5 us (16%)
  local copies, waits for them, and re-layouts  55.4 us (9%)
  between operations  13.8 us (2%)
  starting transfers between devices  9.73 us (2%)
  loops' own time  8.8 us (1%)
    psum x1, waiting for transfers between devices, on_device(): whole_sum = lax.psum(lag_stack, 'seg')  160 us
    psum x1, waiting for transfers between devices, on_device(): lax.psum(picked_real, 'chan').astype(jnp.float32)  107 us
    another operation x4, other arithmetic  90.6 us
    concatenate x4, other arithmetic, correlate(): jnp.concatenate([cross_real, cross_imag], axis=-1).astype(jnp.bfloat16)  65.8 us
    while x2, local copies, waits for them, and re-layouts, on_device(): lax.map(correlate, starts).reshape(ch_local, sources_count, LAGS)  26.9 us
    dot_general x4, matrix products, correlate(): jnp.einsum('wck,wsk->csk', part_imag, source_imag, preferred_element_type...  23.8 us
    dot_general x4, matrix products, correlate(): jnp.einsum('wck,wsk->csk', part_real, source_real, preferred_element_type...  23.5 us
    dot_general x4, matrix products, correlate(): product = jnp.dot(joined, lag_table, preferred_element_type=jnp.float32)  15.9 us
  transfers between devices with their start and end apart: 3, of which 2 were waited for; matrix products, arithmetic and copies ran while one was open for 15% of the time, Pallas kernels for 0%

commit v1 on v0

v1 whole, which is shorter than its diff:
```python
import math

import jax
import jax.numpy as jnp
import numpy as np
from jax import lax
from jax.experimental import pallas as pl
from jax.experimental.pallas import tpu as pltpu
from jax.sharding import PartitionSpec as P

W = 4096
NF = 1152
FIRST_BIN = 16
SMOOTH = 64
MAXLAG = 256
LAGS = 512
VS = 128
CHAN = 32
SEG = 4
WIN = 12
CH = 32
NKB = NF // 128
ROWS_MAIN = WIN * CH
ROWS_SRC = 48
ROWS = ROWS_MAIN + ROWS_SRC
MESH = pl.DeviceIdType.MESH
BF = jnp.bfloat16
F32 = jnp.float32


def unit(product):
    phase = np.mod(product, W).astype(np.float64) * (2.0 * math.pi / W)
    return np.cos(phase).astype(np.float32), np.sin(phase).astype(np.float32)


def small_tables():
    freqs = FIRST_BIN + np.arange(NF)
    coarse = unit(64 * np.arange(64)[:, None] * freqs[None, :128])
    fine = unit(np.arange(64)[:, None] * freqs[None, :])
    lag_coarse = unit(64 * (np.arange(8)[:, None] - 4) * freqs[None, :128])
    width = np.abs(np.arange(NF)[:, None] - np.arange(NF)[None, :]) <= SMOOTH
    inverse = (1.0 / width.sum(axis=0)).astype(np.float32).reshape(1, NF)
    return coarse, fine, lag_coarse, inverse


def slot_masks(rows):
    lane = lax.broadcasted_iota(jnp.int32, (rows, 128), 1)
    return [((lane // 8) // (1 << b)) % 2 == 1 for b in range(4)]


def interleave(values, masks):
    zero = jnp.zeros_like(values[0])
    state = [pltpu.roll(v, 8 * w, 1) if w else v for w, v in enumerate(values)]
    state = state + [zero] * (16 - len(state))
    for b in range(4):
        state = [
            jnp.where(masks[b], state[(i + (1 << b)) % 16], state[i]) for i in range(16)
        ]
    return [state[(-m) % 16] for m in range(16)]


def spectra_kernel(
    x_ref, wl_ref, sc_ref, ca_ref, sa_ref, cb_ref, sb_ref, inv_ref,
    a_out, b_out,
    xv, xs, rm, rs, tab, lhs, acc, magp,
    ssem, rsem, ssem2, rsem2, lsem,
):
    me = lax.axis_index("chan")
    core = lax.rem(me, 2)
    load = pltpu.make_async_copy(x_ref, xv, lsem.at[0])
    load.start()
    barrier = pltpu.get_barrier_semaphore()

    def greet(d, _):
        pl.semaphore_signal(
            barrier, inc=1, device_id={"chan": lax.rem(me + d, CHAN)}, device_id_type=MESH
        )
        return 0

    lax.fori_loop(1, CHAN, greet, 0)
    pl.semaphore_wait(barrier, CHAN - 1)

    def main_copy(d, source):
        peer = lax.rem(me + d, CHAN)
        return pltpu.make_async_remote_copy(
            src_ref=x_ref.at[:, pl.ds(peer * CH, CH), :],
            dst_ref=rm.at[source],
            send_sem=ssem.at[d],
            recv_sem=rsem.at[source],
            device_id={"chan": peer},
            device_id_type=MESH,
        )

    def src_copy(d, source):
        peer = lax.rem(me + d, CHAN)
        return pltpu.make_async_remote_copy(
            src_ref=xs.at[peer],
            dst_ref=rs.at[source],
            send_sem=ssem2.at[d],
            recv_sem=rsem2.at[source],
            device_id={"chan": peer},
            device_id_type=MESH,
        )

    def send(d, _):
        main_copy(d, me).start()
        return 0

    lax.fori_loop(1, CHAN, send, 0)
    own = pltpu.make_async_copy(x_ref.at[:, pl.ds(me * CH, CH), :], rm.at[me], lsem.at[1])
    own.start()

    load.wait()
    hot = (
        lax.broadcasted_iota(jnp.int32, (VS, CHAN * CH), 1) == sc_ref[...]
    ).astype(F32).astype(BF)

    def pick(pair, _):
        first = jnp.dot(hot, xv[2 * pair], preferred_element_type=F32)
        second = jnp.dot(hot, xv[2 * pair + 1], preferred_element_type=F32)
        half = pair // 3
        row = pl.multiple_of(lax.rem(pair, 3) * 16, 16)
        for q in range(16):
            both = jnp.concatenate([first[8 * q:8 * q + 8], second[8 * q:8 * q + 8]], axis=0)
            xs[2 * q + half, pl.ds(row, 16), :] = both.astype(BF)
        return 0

    lax.fori_loop(0, WIN // 2, pick, 0)

    def send_src(d, _):
        src_copy(d, me).start()
        return 0

    lax.fori_loop(1, CHAN, send_src, 0)
    own2 = pltpu.make_async_copy(xs.at[me], rs.at[me], lsem.at[2])
    own2.start()

    def make_rows(a, _):
        row = pl.multiple_of(a * 64, 64)
        ca = jnp.broadcast_to(ca_ref[pl.ds(a, 1), :], (64, 128))
        sa = jnp.broadcast_to(sa_ref[pl.ds(a, 1), :], (64, 128))
        for kb in range(NKB):
            cb = cb_ref[:, kb * 128:kb * 128 + 128]
            sb = sb_ref[:, kb * 128:kb * 128 + 128]
            tab[pl.ds(row, 64), kb * 128:kb * 128 + 128] = (ca * cb - sa * sb).astype(BF)
            tab[pl.ds(row, 64), NF + kb * 128:NF + kb * 128 + 128] = (
                -(sa * cb + ca * sb)
            ).astype(BF)
        return 0

    lax.fori_loop(0, 64, make_rows, 0)
    acc[...] = jnp.zeros_like(acc)
    own.wait()
    own2.wait()

    lane = lax.broadcasted_iota(jnp.int32, (1, 128), 1)

    def gather_group(step, _):
        group = lax.rem(me // 4 + CHAN // 4 - step, CHAN // 4)
        for i in range(4):
            j = group * 4 + i

            @pl.when(j != me)
            def _():
                main_copy(0, j).wait_recv()
                src_copy(0, j).wait_recv()

            def keep(w):
                inside = lane + j * 128 < wl_ref[w]
                return jnp.where(inside, 1.0, 0.0).astype(BF)

            for w in range(WIN):
                lhs[w * CH:(w + 1) * CH, i * 128:(i + 1) * 128] = rm[j, w] * keep(w)
            for t in range(3):
                upper = jnp.broadcast_to(keep(core * 6 + 2 * t).astype(F32), (8, 128))
                lower = jnp.broadcast_to(keep(core * 6 + 2 * t + 1).astype(F32), (8, 128))
                both = jnp.concatenate([upper, lower], axis=0).astype(BF)
                lhs[ROWS_MAIN + 16 * t:ROWS_MAIN + 16 * t + 16, i * 128:(i + 1) * 128] = (
                    rs[j, 16 * t:16 * t + 16, :] * both
                )

        def column(ct, _):
            col = pl.multiple_of(ct * 256, 256)
            row = pl.multiple_of(group * 512, 512)
            acc[:, pl.ds(col, 256)] += jnp.dot(
                lhs[...], tab[pl.ds(row, 512), pl.ds(col, 256)], preferred_element_type=F32
            )
            return 0

        lax.fori_loop(0, 2 * NF // 256, column, 0)
        return 0

    lax.fori_loop(0, CHAN // 4, gather_group, 0)

    def sent(d, _):
        main_copy(d, me).wait_send()
        src_copy(d, me).wait_send()
        return 0

    lax.fori_loop(1, CHAN, sent, 0)

    magp[:, 0:128] = jnp.zeros((ROWS, 128), BF)
    magp[:, NF + 128:NF + 256] = jnp.zeros((ROWS, 128), BF)

    def magnitude(kb, _):
        col = pl.multiple_of(kb * 128, 128)
        re = acc[:, pl.ds(col, 128)]
        im = acc[:, pl.ds(pl.multiple_of(NF + col, 128), 128)]
        magp[:, pl.ds(pl.multiple_of(col + 128, 128), 128)] = jnp.sqrt(re * re + im * im).astype(BF)
        return 0

    lax.fori_loop(0, NKB, magnitude, 0)
    band = (
        jnp.abs(
            lax.broadcasted_iota(jnp.int32, (384, 128), 0)
            - 128
            - lax.broadcasted_iota(jnp.int32, (384, 128), 1)
        )
        <= SMOOTH
    ).astype(F32).astype(BF)

    def whiten(kb, _):
        col = pl.multiple_of(kb * 128, 128)
        col2 = pl.multiple_of(NF + col, 128)
        total = jnp.dot(magp[:, pl.ds(col, 384)], band, preferred_element_type=F32)
        scale = 1.0 / (total * inv_ref[:, pl.ds(col, 128)] + 1e-06)
        acc[:, pl.ds(col, 128)] = acc[:, pl.ds(col, 128)] * scale
        acc[:, pl.ds(col2, 128)] = acc[:, pl.ds(col2, 128)] * scale
        return 0

    lax.fori_loop(0, NKB, whiten, 0)

    b_out[...] = acc[ROWS_MAIN:, :].astype(BF)
    masks = slot_masks(8)

    def spread(step, _):
        kb = step // 4
        c8 = pl.multiple_of(lax.rem(step, 4) * 8, 8)
        for ri in range(2):
            col = pl.multiple_of(ri * NF + kb * 128, 128)
            values = [
                acc[pl.ds(pl.multiple_of(w * CH + c8, 8), 8), pl.ds(col, 128)] for w in range(WIN)
            ]
            for m, out in enumerate(interleave(values, masks)):
                a_out[kb * 16 + m, ri, pl.ds(c8, 8), :] = out
        return 0

    lax.fori_loop(0, NKB * 4, spread, 0)


def spectra(x, wl, sc, tables):
    (ca, sa), (cb, sb), _, inverse = tables
    vmem = pl.BlockSpec(memory_space=pltpu.VMEM)
    return pl.pallas_call(
        spectra_kernel,
        out_shape=(
            jax.ShapeDtypeStruct((NKB * 16, 2, CH, 128), F32),
            jax.ShapeDtypeStruct((ROWS_SRC, 2 * NF), BF),
        ),
        in_specs=[
            pl.BlockSpec(memory_space=pl.ANY),
            pl.BlockSpec(memory_space=pltpu.SMEM),
            vmem, vmem, vmem, vmem, vmem, vmem,
        ],
        out_specs=(vmem, vmem),
        scratch_shapes=[
            pltpu.VMEM((WIN, CHAN * CH, 128), BF),
            pltpu.VMEM((CHAN, ROWS_SRC, 128), BF),
            pltpu.VMEM((CHAN, WIN, CH, 128), BF),
            pltpu.VMEM((CHAN, ROWS_SRC, 128), BF),
            pltpu.VMEM((W, 2 * NF), BF),
            pltpu.VMEM((ROWS, 512), BF),
            pltpu.VMEM((ROWS, 2 * NF), F32),
            pltpu.VMEM((ROWS, NF + 256), BF),
            pltpu.SemaphoreType.DMA((CHAN,)),
            pltpu.SemaphoreType.DMA((CHAN,)),
            pltpu.SemaphoreType.DMA((CHAN,)),
            pltpu.SemaphoreType.DMA((CHAN,)),
            pltpu.SemaphoreType.DMA((3,)),
        ],
        compiler_params=pltpu.CompilerParams(
            collective_id=0, has_side_effects=True, vmem_limit_bytes=60 * 1024 * 1024
        ),
        name="spectra",
    )(x, wl, sc.reshape(VS, 1), ca, sa, cb, sb, inverse)


def cross_kernel(a_ref, b_ref, la_ref, ls_ref, cb_ref, sb_ref, out_ref, bi, xk, tt):
    for a in range(8):
        ca = jnp.broadcast_to(la_ref[a:a + 1, :], (64, 128))
        sa = jnp.broadcast_to(ls_ref[a:a + 1, :], (64, 128))
        for kb in range(NKB):
            cols = slice(kb * 128, kb * 128 + 128)
            cols2 = slice(NF + kb * 128, NF + kb * 128 + 128)
            cb, sb = cb_ref[:, cols], sb_ref[:, cols]
            tt[a * 64:a * 64 + 64, cols] = (ca * cb - sa * sb).astype(BF)
            tt[a * 64:a * 64 + 64, cols2] = (-(sa * cb + ca * sb)).astype(BF)

    masks = slot_masks(8)
    diagonal = (
        lax.rem(lax.broadcasted_iota(jnp.int32, (8, 128), 1), 8)
        == lax.broadcasted_iota(jnp.int32, (8, 128), 0)
    )

    def block(kb, _):
        def spread(q, _):
            row = pl.multiple_of(q * 8, 8)
            for ri in range(2):
                col = pl.multiple_of(ri * NF + kb * 128, 128)
                values = []
                for half in range(2):
                    for t in range(3):
                        pair = b_ref[2 * q + half, 16 * t:16 * t + 16, pl.ds(col, 128)].astype(F32)
                        values += [pair[:8], pair[8:]]
                for m, out in enumerate(interleave(values, masks)):
                    bi[m, ri, pl.ds(row, 8), :] = out
            return 0

        lax.fori_loop(0, 16, spread, 0)

        def pair_of_groups(mp, _):
            products = []
            for half in range(2):
                m = 2 * mp + half
                group = kb * 16 + m
                sides = []
                for ri in range(2):
                    tiles = [
                        jnp.where(
                            diagonal,
                            jnp.broadcast_to(a_ref[group, ri, c:c + 1, :], (8, 128)),
                            0.0,
                        )
                        for c in range(CH)
                    ]
                    sides.append(jnp.concatenate(tiles, axis=0).astype(BF))
                left = jnp.concatenate(sides, axis=1)
                bre, bim = bi[m, 0], bi[m, 1]
                right = jnp.concatenate(
                    [
                        jnp.concatenate([bre, bim], axis=1),
                        jnp.concatenate([-bim, bre], axis=1),
                    ],
                    axis=0,
                ).astype(BF)
                products.append(
                    lax.dot_general(
                        left, right, (((1,), (1,)), ((), ())), preferred_element_type=F32
                    )
                )
            row = pl.multiple_of(kb * 128 + mp * 16, 16)
            for ri in range(2):
                for c in range(CH):
                    both = jnp.concatenate(
                        [p[c * 8:c * 8 + 8, ri * 128:ri * 128 + 128] for p in products], axis=0
                    )
                    xk[pl.ds(pl.multiple_of(ri * NF + row, 16), 16), c * 128:c * 128 + 128] = both.astype(BF)
            return 0

        lax.fori_loop(0, 8, pair_of_groups, 0)
        return 0

    lax.fori_loop(0, NKB, block, 0)

    def lags(cb, _):
        col = pl.multiple_of(cb * 256, 256)
        result = jnp.dot(tt[...], xk[:, pl.ds(col, 256)], preferred_element_type=F32)
        for i in range(2):
            flipped = result[:, i * 128:i * 128 + 128].T
            for g in range(SEG):
                out_ref[g, 2 * cb + i] = flipped[32 * g:32 * g + 32].astype(BF)
        return 0

    lax.fori_loop(0, CH // 2, lags, 0)


def cross(a, b, tables):
    _, (cb, sb), (la, ls), _ = tables
    vmem = pl.BlockSpec(memory_space=pltpu.VMEM)
    return pl.pallas_call(
        cross_kernel,
        out_shape=jax.ShapeDtypeStruct((SEG, CH, VS // SEG, LAGS), BF),
        in_specs=[vmem] * 6,
        out_specs=vmem,
        scratch_shapes=[
            pltpu.VMEM((16, 2, VS, 128), F32),
            pltpu.VMEM((2 * NF, CH * VS), BF),
            pltpu.VMEM((LAGS, 2 * NF), BF),
        ],
        compiler_params=pltpu.CompilerParams(vmem_limit_bytes=60 * 1024 * 1024),
        name="cross",
    )(a, b, la, ls, cb, sb)


def on_device(strain_rate, window_length, source_channel):
    tables = small_tables()
    tables = jax.tree.map(jnp.asarray, tables)
    a, b = spectra(strain_rate, window_length, source_channel, tables)
    gathered = lax.all_gather(b, "chan", axis=0, tiled=False)
    shares = cross(a, gathered, tables)
    received = lax.all_to_all(shares, "seg", split_axis=0, concat_axis=0, tiled=True)
    scale = 1.0 / math.sqrt(NF * WIN * SEG)
    return jnp.sum(received.astype(F32), axis=0) * scale


def solution(mesh):
    in_specs = (P("seg", None, "chan"), P("seg"), P())
    out_specs = P("chan", "seg", None)
    return jax.shard_map(
        on_device, mesh=mesh, in_specs=in_specs, out_specs=out_specs, check_vma=False
    )
```

time: 627 us -> 270 us (0.43)
  waiting for transfers between devices: 266 us -> 47.9 us
  other arithmetic: 168 us -> 2.37 us
  Pallas kernels: 0 us -> 153 us
  matrix products: 99.5 us -> 0 us
  local copies, waits for them, and re-layouts: 55.4 us -> 1.39 us
  blocking collectives: 0 us -> 52.3 us
  starting transfers between devices: 9.73 us -> 0.01 us
  loops' own time: 8.8 us -> 0 us
    psum x2 -> x0, waiting for transfers between devices: 266 us -> none  [the longest x1 160 us: on_device(): whole_sum = lax.psum(lag_stack, 'seg')]
    pallas_call x0 -> x2, Pallas kernels: none -> 153 us  [the longest x1 96.9 us: spectra(): pl.pallas_call(spectra_kernel, out_shape=(jax.ShapeDtypeStruct((NKB * 16,...]
    dot_general x26 -> x0, matrix products: 99.5 us -> none  [the longest x4 23.8 us: correlate(): jnp.einsum('wck,wsk->csk', part_imag, source_imag, preferred_element_type...]
    another operation x4 -> x0, other arithmetic: 90.6 us -> none
    concatenate x5 -> x0, other arithmetic: 67.5 us -> none  [the longest x4 65.8 us: correlate(): jnp.concatenate([cross_real, cross_imag], axis=-1).astype(jnp.bfloat16)]
    all_to_all x0 -> x1, blocking collectives: none -> 52.3 us  [on_device(): lax.all_to_all(shares, 'seg', split_axis=0, concat_axis=0, tiled=True)]
    all_gather x0 -> x1, waiting for transfers between devices: none -> 47.8 us  [on_device(): gathered = lax.all_gather(b, 'chan', axis=0, tiled=False)]
    while x66 -> x0, local copies, waits for them, and re-layouts: 27 us -> none  [the longest x2 26.9 us: on_device(): lax.map(correlate, starts).reshape(ch_local, sources_count, LAGS)]
  transfers between devices with their start and end apart: 3 -> 1, of which waited for: 2 -> 1; matrix products, arithmetic and copies ran while one was open for 15% -> 0% of each run, Pallas kernels for 0% -> 0%
where the time goes in v1:
time: 270 us
  Pallas kernels  153 us (57%)
  blocking collectives  52.3 us (19%)
  waiting for transfers between devices  47.9 us (18%)
  between operations  13.4 us (5%)
    pallas_call x1, Pallas kernels, spectra(): pl.pallas_call(spectra_kernel, out_shape=(jax.ShapeDtypeStruct((NKB * 16,...  96.9 us
    pallas_call x1, Pallas kernels, cross(): pl.pallas_call(cross_kernel, out_shape=jax.ShapeDtypeStruct((SEG, CH, VS...  55.8 us
    all_to_all x1, blocking collectives, on_device(): lax.all_to_all(shares, 'seg', split_axis=0, concat_axis=0, tiled=True)  52.3 us
    all_gather x1, waiting for transfers between devices, on_device(): gathered = lax.all_gather(b, 'chan', axis=0, tiled=False)  47.8 us
  transfers between devices with their start and end apart: 1, of which 1 were waited for; matrix products, arithmetic and copies ran while one was open for 0% of the time, Pallas kernels for 0%

profile of v1, /device:TPU:1, one launch (start us, length us, event | category | flops | bytes accessed | tf_op | source)
XLA Modules:
  0.0 269.9 jit_solution(5110673563685978823)
XLA Ops:
  6.5 0.0 all-gather.3.cloned.1.call-start
  6.5 1.4 copy.11.sc_ref
  7.9 96.9 %spectra.1 = (f32[144,2,32,128]{3,2,1,0:T(8,128)}, bf16[48,2304]{1,0:T(8,128)(2,1)}) custom-call(bf16[12,1024,128]{2,1,0:T(8,128)(2,1)} %x_ref.1, s32[12]{0:T(128)} %wl_ref.1, s32[128,1]{1,0:T(8,128)} %copy.11.sc_ref, f32[64,128]{1,0:T(8,128)} %constant.18.clone.ca_ref, f32[64,128]{1,0:T(8,128)} %constant.19.clone.sa_ref, f32[64,1152]{1,0:T(8,128)} %constant.20.clone.cb_ref, ...), custom_call_target="tpu_custom_call" | custom-call | tf_op jit(solution)/shard_map/spectra/pallas_call | solution.py:254
  104.8 0.0 all-gather.3.cloned.1.call-update
  104.8 47.8 %all-gather.3.cloned.1.call-done = bf16[1536,2304]{1,0:T(8,128)(2,1)} async-done(((bf16[48,2304]{1,0:T(8,128)(2,1)}), bf16[1536,2304]{1,0:T(8,128)(2,1)}) %all-gather.3.cloned.1.call-update) | async-done | bytes 7077904 | tf_op jit(solution)/shard_map/all_gather | solution.py:399
  152.7 55.8 %cross.1 = bf16[4,32,32,512]{3,2,1,0:T(8,128)(2,1)} custom-call(f32[144,2,32,128]{3,2,1,0:T(8,128)} %get-tuple-element.7.a_ref, bf16[32,48,2304]{2,1,0:T(8,128)(2,1)} %bitcast.2, f32[8,128]{1,0:T(8,128)} %constant.22.clone.la_ref, f32[8,128]{1,0:T(8,128)} %constant.23.clone.ls_ref, f32[64,1152]{1,0:T(8,128)} %constant.20.clone.cb_ref, ...), custom_call_target="tpu_custom_call" | custom-call | tf_op jit(solution)/shard_map/cross/pallas_call | solution.py:380
  208.4 52.3 %all_to_all.5 = bf16[4,32,32,512]{3,2,1,0:T(8,128)(2,1)S(1)} all-to-all(bf16[4,32,32,512]{3,2,1,0:T(8,128)(2,1)} %cross.1), channel_id=1, replica_groups=mesh['seg'=4,'chan'=32] {'seg'}, dimensions={0} | all-to-all | bytes 8388608 | tf_op jit(solution)/shard_map/all_to_all | solution.py:401
  260.7 0.8 convert_reduce_fusion
  261.5 1.6 broadcast_multiply_fusion
Async XLA Ops:
  6.5 146.1 %all-gather.3.cloned.1.call-start = ((), (), s32[]{:S(2)}) async-start(), calls=%async_computation.1 | async-start | bytes 7299072 | tf_op jit(solution)/shard_map/all_gather | solution.py:399
Sparse Core Ops, SparseCore 0:
  105.0 47.6 all-gather.2

commit v2 on v1

--- a/solution.py
+++ b/solution.py
@@ -285,7 +285,82 @@
     )(x, wl, sc.reshape(VS, 1), ca, sa, cb, sb, inverse)
 
 
-def cross_kernel(a_ref, b_ref, la_ref, ls_ref, cb_ref, sb_ref, out_ref, bi, xk, tt):
+NC = 3
+CKB = NKB // NC
+CL = CKB * 128
+
+
+def cross_kernel(
+    a_hbm, b_hbm, la_ref, ls_ref, cb_ref, sb_ref, out_ref,
+    a_ref, g_ref, bi, xk, tt, mine, share, landed,
+    s1, r1, s2, r2, s3, r3, s4, r4, sx, rx, lsem,
+):
+    me = lax.axis_index("chan")
+    seg = lax.axis_index("seg")
+    z, y, core = me // 8, lax.rem(me // 2, 4), lax.rem(me, 2)
+    load = pltpu.make_async_copy(a_hbm, a_ref, lsem.at[0])
+    load.start()
+
+    def at(zz, yy, cc):
+        return {"chan": lax.rem(zz + 4, 4) * 8 + lax.rem(yy + 4, 4) * 2 + cc}
+
+    def beyond(axis, d):
+        return at(z + d, y, core) if axis == 0 else at(z, y + d, core)
+
+    def segment(d):
+        return {"seg": lax.rem(seg + d, SEG)}
+
+    barrier = pltpu.get_barrier_semaphore()
+    for d in (1, 2, 3):
+        for who in (beyond(0, d), beyond(1, d), segment(d)):
+            pl.semaphore_signal(barrier, inc=1, device_id=who, device_id_type=MESH)
+    pl.semaphore_signal(barrier, inc=1, device_id=at(z, y, 1 - core), device_id_type=MESH)
+    pl.semaphore_wait(barrier, 10)
+
+    def remote(src, dst, send, recv, who):
+        return pltpu.make_async_remote_copy(
+            src_ref=src, dst_ref=dst, send_sem=send, recv_sem=recv, device_id=who, device_id_type=MESH
+        )
+
+    def block(ch, ri):
+        return b_hbm.at[:, ri * NF + ch * CL:ri * NF + (ch + 1) * CL]
+
+    def first(ch, ri, d):
+        k = (ch * 2 + ri) * 3 + d - 1
+        return remote(block(ch, ri), g_ref.at[ch, ri, core, z, y], s1.at[k], r1.at[k], beyond(ri, d))
+
+    def line(ch, ri, start, size, d):
+        if ri == 0:
+            return g_ref.at[ch, ri, core, start:start + size, lax.rem(y + d + 4, 4)]
+        return g_ref.at[ch, ri, core, lax.rem(z + d + 4, 4), start:start + size]
+
+    def second(ch, ri, way):
+        k = (ch * 2 + ri) * 2 + way
+        d = 1 if way == 0 else 3
+        whole = line(ch, ri, 0, 4, 0)
+        return remote(whole, whole, s2.at[k], r2.at[k], beyond(1 - ri, d))
+
+    def third(ch, ri, way):
+        k = (ch * 2 + ri) * 2 + way
+        d = 1 if way == 0 else 3
+        part = line(ch, ri, 2 * way, 2, -1 if way == 0 else 1)
+        return remote(part, part, s3.at[k], r3.at[k], beyond(1 - ri, d))
+
+    def fourth(ch, ri):
+        k = ch * 2 + ri
+        part = g_ref.at[ch, ri, core]
+        return remote(part, part, s4.at[k], r4.at[k], at(z, y, 1 - core))
+
+    def own(ch, ri):
+        return pltpu.make_async_copy(block(ch, ri), g_ref.at[ch, ri, core, z, y], lsem.at[1 + ch * 2 + ri])
+
+    halves = (0, 1)
+    for ch in range(NC):
+        for ri in halves:
+            for d in (2, 1, 3):
+                first(ch, ri, d).start()
+            own(ch, ri).start()
+
     for a in range(8):
         ca = jnp.broadcast_to(la_ref[a:a + 1, :], (64, 128))
         sa = jnp.broadcast_to(ls_ref[a:a + 1, :], (64, 128))
@@ -302,15 +377,43 @@
         == lax.broadcasted_iota(jnp.int32, (8, 128), 0)
     )
 
-    def block(kb, _):
+    def step_second(ch):
+        for ri in halves:
+            for d in (1, 2, 3):
+                first(ch, ri, d).wait_recv()
+            own(ch, ri).wait()
+            for way in (0, 1):
+                second(ch, ri, way).start()
+
+    def step_third(ch):
+        for ri in halves:
+            for way in (0, 1):
+                second(ch, ri, way).wait_recv()
+                third(ch, ri, way).start()
+
+    def step_fourth(ch):
+        for ri in halves:
+            for way in (0, 1):
+                third(ch, ri, way).wait_recv()
+            fourth(ch, ri).start()
+
+    def arrived(ch):
+        for ri in halves:
+            fourth(ch, ri).wait_recv()
+
+    def bins(ch, kbl):
+        kb = ch * CKB + kbl
+
         def spread(q, _):
             row = pl.multiple_of(q * 8, 8)
             for ri in range(2):
-                col = pl.multiple_of(ri * NF + kb * 128, 128)
+                col = kbl * 128
                 values = []
                 for half in range(2):
                     for t in range(3):
-                        pair = b_ref[2 * q + half, 16 * t:16 * t + 16, pl.ds(col, 128)].astype(F32)
+                        pair = g_ref[
+                            ch, ri, half, q // 4, lax.rem(q, 4), 16 * t:16 * t + 16, col:col + 128
+                        ].astype(F32)
                         values += [pair[:8], pair[8:]]
                 for m, out in enumerate(interleave(values, masks)):
                     bi[m, ri, pl.ds(row, 8), :] = out
@@ -358,49 +461,124 @@
             return 0
 
         lax.fori_loop(0, 8, pair_of_groups, 0)
-        return 0
-
-    lax.fori_loop(0, NKB, block, 0)
-
-    def lags(cb, _):
-        col = pl.multiple_of(cb * 256, 256)
-        result = jnp.dot(tt[...], xk[:, pl.ds(col, 256)], preferred_element_type=F32)
-        for i in range(2):
-            flipped = result[:, i * 128:i * 128 + 128].T
-            for g in range(SEG):
-                out_ref[g, 2 * cb + i] = flipped[32 * g:32 * g + 32].astype(BF)
-        return 0
-
-    lax.fori_loop(0, CH // 2, lags, 0)
+
+    for ch in range(NC):
+        step_second(ch)
+    step_third(0)
+    step_third(1)
+    step_fourth(0)
+    load.wait()
+    arrived(0)
+    bins(0, 0)
+    step_third(2)
+    step_fourth(1)
+    bins(0, 1)
+    step_fourth(2)
+    bins(0, 2)
+    for ch in range(1, NC):
+        arrived(ch)
+        for kbl in range(CKB):
+            bins(ch, kbl)
+
+    def exchange(block4, d):
+        c0 = pl.multiple_of(block4 * 4, 4)
+        return remote(
+            share.at[lax.rem(seg + d, SEG), pl.ds(c0, 4)],
+            landed.at[d - 1, pl.ds(c0, 4)],
+            sx.at[d - 1, block4],
+            rx.at[d - 1, block4],
+            segment(d),
+        )
+
+    def lags(block4, _):
+        for i2 in range(2):
+            cb = block4 * 2 + i2
+            col = pl.multiple_of(cb * 256, 256)
+            result = jnp.dot(tt[...], xk[:, pl.ds(col, 256)], preferred_element_type=F32)
+            for i in range(2):
+                flipped = result[:, i * 128:i * 128 + 128].T
+                for g in range(SEG):
+                    part = flipped[32 * g:32 * g + 32]
+                    share[g, 2 * cb + i] = part.astype(BF)
+
+                    @pl.when(seg == g)
+                    def _():
+                        mine[2 * cb + i] = part
+
+        for d in (2, 1, 3):
+            exchange(block4, d).start()
+        return 0
+
+    lax.fori_loop(0, CH // 4, lags, 0)
+
+    scale = 1.0 / math.sqrt(NF * WIN * SEG)
+
+    def finish(block4, _):
+        for d in (1, 2, 3):
+            exchange(block4, d).wait_recv()
+        c0 = pl.multiple_of(block4 * 4, 4)
+        total = mine[pl.ds(c0, 4)]
+        for d in (1, 2, 3):
+            total = total + landed[d - 1, pl.ds(c0, 4)].astype(F32)
+        out_ref[pl.ds(c0, 4)] = total * scale
+        return 0
+
+    lax.fori_loop(0, CH // 4, finish, 0)
+
+    for ch in range(NC):
+        for ri in halves:
+            for d in (1, 2, 3):
+                first(ch, ri, d).wait_send()
+            for way in (0, 1):
+                second(ch, ri, way).wait_send()
+                third(ch, ri, way).wait_send()
+            fourth(ch, ri).wait_send()
+
+    def sent(block4, _):
+        for d in (1, 2, 3):
+            exchange(block4, d).wait_send()
+        return 0
+
+    lax.fori_loop(0, CH // 4, sent, 0)
 
 
 def cross(a, b, tables):
     _, (cb, sb), (la, ls), _ = tables
     vmem = pl.BlockSpec(memory_space=pltpu.VMEM)
+    hbm = pl.BlockSpec(memory_space=pl.ANY)
+    dma = pltpu.SemaphoreType.DMA
     return pl.pallas_call(
         cross_kernel,
-        out_shape=jax.ShapeDtypeStruct((SEG, CH, VS // SEG, LAGS), BF),
-        in_specs=[vmem] * 6,
+        out_shape=jax.ShapeDtypeStruct((CH, VS // SEG, LAGS), F32),
+        in_specs=[hbm, hbm] + [vmem] * 4,
         out_specs=vmem,
         scratch_shapes=[
+            pltpu.VMEM((NKB * 16, 2, CH, 128), F32),
+            pltpu.VMEM((NC, 2, 2, 4, 4, ROWS_SRC, CL), BF),
             pltpu.VMEM((16, 2, VS, 128), F32),
             pltpu.VMEM((2 * NF, CH * VS), BF),
             pltpu.VMEM((LAGS, 2 * NF), BF),
+            pltpu.VMEM((CH, VS // SEG, LAGS), F32),
+            pltpu.VMEM((SEG, CH, VS // SEG, LAGS), BF),
+            pltpu.VMEM((SEG - 1, CH, VS // SEG, LAGS), BF),
+            dma((NC * 6,)), dma((NC * 6,)),
+            dma((NC * 4,)), dma((NC * 4,)),
+            dma((NC * 4,)), dma((NC * 4,)),
+            dma((NC * 2,)), dma((NC * 2,)),
+            dma((SEG - 1, CH // 4)), dma((SEG - 1, CH // 4)),
+            dma((1 + NC * 2,)),
         ],
-        compiler_params=pltpu.CompilerParams(vmem_limit_bytes=60 * 1024 * 1024),
+        compiler_params=pltpu.CompilerParams(
+            collective_id=1, has_side_effects=True, vmem_limit_bytes=60 * 1024 * 1024
+        ),
         name="cross",
     )(a, b, la, ls, cb, sb)
 
 
 def on_device(strain_rate, window_length, source_channel):
-    tables = small_tables()
-    tables = jax.tree.map(jnp.asarray, tables)
+    tables = jax.tree.map(jnp.asarray, small_tables())
     a, b = spectra(strain_rate, window_length, source_channel, tables)
-    gathered = lax.all_gather(b, "chan", axis=0, tiled=False)
-    shares = cross(a, gathered, tables)
-    received = lax.all_to_all(shares, "seg", split_axis=0, concat_axis=0, tiled=True)
-    scale = 1.0 / math.sqrt(NF * WIN * SEG)
-    return jnp.sum(received.astype(F32), axis=0) * scale
+    return cross(a, b, tables)
 
 
 def solution(mesh):

time: 270 us -> 214 us (0.79)
  Pallas kernels: 153 us -> 210 us
  blocking collectives: 52.3 us -> 0 us
  waiting for transfers between devices: 47.9 us -> 0 us
  between operations: 13.4 us -> 0.02 us
  local copies, waits for them, and re-layouts: 1.39 us -> 4.57 us
    pallas_call x1, Pallas kernels: 55.8 us -> 113 us  [cross(): pl.pallas_call(cross_kernel, out_shape=jax.ShapeDtypeStruct((CH, VS // SE...]
    all_to_all x1 -> x0, blocking collectives: 52.3 us -> none  [on_device(): lax.all_to_all(shares, 'seg', split_axis=0, concat_axis=0, tiled=True)]
    all_gather x1 -> x0, waiting for transfers between devices: 47.8 us -> none  [on_device(): gathered = lax.all_gather(b, 'chan', axis=0, tiled=False)]
    unnamed x0 -> x1, local copies, waits for them, and re-layouts: none -> 3.19 us
  transfers between devices with their start and end apart: 1 -> 0, of which waited for: 1 -> 0; matrix products, arithmetic and copies ran while one was open for 0% -> 0% of each run, Pallas kernels for 0% -> 0%
where the time goes in v2:
time: 214 us
  Pallas kernels  210 us (98%)
  local copies, waits for them, and re-layouts  4.57 us (2%)
    pallas_call x1, Pallas kernels, cross(): pl.pallas_call(cross_kernel, out_shape=jax.ShapeDtypeStruct((CH, VS // SE...  113 us
    pallas_call x1, Pallas kernels, spectra(): pl.pallas_call(spectra_kernel, out_shape=(jax.ShapeDtypeStruct((NKB * 16,...  96.8 us

profile of v2, /device:TPU:1, one launch (start us, length us, event | category | flops | bytes accessed | tf_op | source)
XLA Modules:
  0.0 214.2 jit_solution(8223578151408058836)
XLA Ops:
  0.0 1.4 copy.11.sc_ref
  1.4 96.8 %spectra.1 = (f32[144,2,32,128]{3,2,1,0:T(8,128)}, bf16[48,2304]{1,0:T(8,128)(2,1)}) custom-call(bf16[12,1024,128]{2,1,0:T(8,128)(2,1)} %x_ref.1, s32[12]{0:T(128)} %wl_ref.1, s32[128,1]{1,0:T(8,128)} %copy.11.sc_ref, f32[64,128]{1,0:T(8,128)} %constant.14.clone.ca_ref, f32[64,128]{1,0:T(8,128)} %constant.15.clone.sa_ref, f32[64,1152]{1,0:T(8,128)} %constant.16.clone.cb_ref, ...), custom_call_target="tpu_custom_call" | custom-call | tf_op jit(solution)/shard_map/spectra/pallas_call | solution.py:254
  98.2 112.8 %cross.1 = f32[32,32,512]{2,1,0:T(8,128)} custom-call(f32[144,2,32,128]{3,2,1,0:T(8,128)} %get-tuple-element.7.a_hbm, bf16[48,2304]{1,0:T(8,128)(2,1)} %get-tuple-element.8.b_hbm, f32[8,128]{1,0:T(8,128)} %constant.18.clone.la_ref, f32[8,128]{1,0:T(8,128)} %constant.19.clone.ls_ref, f32[64,1152]{1,0:T(8,128)} %constant.16.clone.cb_ref, ...), custom_call_target="tpu_custom_call" | custom-call | tf_op jit(solution)/shard_map/cross/pallas_call | solution.py:550
  211.0 3.2 %copy.13 = f32[32,32,512]{2,1,0:T(8,128)} copy(f32[32,32,512]{2,1,0:T(8,128)} %cross.1) | data formatting | bytes 4194304

commit v3 on v2

--- a/solution.py
+++ b/solution.py
@@ -23,6 +23,7 @@
 ROWS_MAIN = WIN * CH
 ROWS_SRC = 48
 ROWS = ROWS_MAIN + ROWS_SRC
+GROUPS = (8, 8, 8, 4, 4)
 MESH = pl.DeviceIdType.MESH
 BF = jnp.bfloat16
 F32 = jnp.float32
@@ -80,34 +81,37 @@
     lax.fori_loop(1, CHAN, greet, 0)
     pl.semaphore_wait(barrier, CHAN - 1)
 
-    def main_copy(d, source):
-        peer = lax.rem(me + d, CHAN)
+    def sender(d):
+        return lax.rem(me + CHAN * 13 - 13 * d, CHAN)
+
+    def main_copy(d):
+        peer = lax.rem(me + 13 * d, CHAN)
         return pltpu.make_async_remote_copy(
             src_ref=x_ref.at[:, pl.ds(peer * CH, CH), :],
-            dst_ref=rm.at[source],
+            dst_ref=rm.at[d],
             send_sem=ssem.at[d],
-            recv_sem=rsem.at[source],
+            recv_sem=rsem.at[d],
             device_id={"chan": peer},
             device_id_type=MESH,
         )
 
-    def src_copy(d, source):
-        peer = lax.rem(me + d, CHAN)
+    def src_copy(d):
+        peer = lax.rem(me + 13 * d, CHAN)
         return pltpu.make_async_remote_copy(
             src_ref=xs.at[peer],
-            dst_ref=rs.at[source],
+            dst_ref=rs.at[d],
             send_sem=ssem2.at[d],
-            recv_sem=rsem2.at[source],
+            recv_sem=rsem2.at[d],
             device_id={"chan": peer},
             device_id_type=MESH,
         )
 
     def send(d, _):
-        main_copy(d, me).start()
-        return 0
-
-    lax.fori_loop(1, CHAN, send, 0)
-    own = pltpu.make_async_copy(x_ref.at[:, pl.ds(me * CH, CH), :], rm.at[me], lsem.at[1])
+        main_copy(d).start()
+        return 0
+
+    lax.fori_loop(1, 8, send, 0)
+    own = pltpu.make_async_copy(x_ref.at[:, pl.ds(me * CH, CH), :], rm.at[0], lsem.at[1])
     own.start()
 
     load.wait()
@@ -128,11 +132,12 @@
     lax.fori_loop(0, WIN // 2, pick, 0)
 
     def send_src(d, _):
-        src_copy(d, me).start()
+        src_copy(d).start()
         return 0
 
     lax.fori_loop(1, CHAN, send_src, 0)
-    own2 = pltpu.make_async_copy(xs.at[me], rs.at[me], lsem.at[2])
+    lax.fori_loop(8, CHAN, send, 0)
+    own2 = pltpu.make_async_copy(xs.at[me], rs.at[0], lsem.at[2])
     own2.start()
 
     def make_rows(a, _):
@@ -149,52 +154,59 @@
         return 0
 
     lax.fori_loop(0, 64, make_rows, 0)
-    acc[...] = jnp.zeros_like(acc)
-    own.wait()
-    own2.wait()
 
     lane = lax.broadcasted_iota(jnp.int32, (1, 128), 1)
 
-    def gather_group(step, _):
-        group = lax.rem(me // 4 + CHAN // 4 - step, CHAN // 4)
-        for i in range(4):
-            j = group * 4 + i
-
-            @pl.when(j != me)
-            def _():
-                main_copy(0, j).wait_recv()
-                src_copy(0, j).wait_recv()
+    def arrive(d, _):
+        main_copy(d).wait_recv()
+        src_copy(d).wait_recv()
+        return 0
+
+    begin = 0
+    for size in GROUPS:
+        if begin == 0:
+            own.wait()
+            own2.wait()
+        lax.fori_loop(max(begin, 1), begin + size, arrive, 0)
+        for i in range(size):
+            d = begin + i
+            j = sender(d)
 
             def keep(w):
                 inside = lane + j * 128 < wl_ref[w]
-                return jnp.where(inside, 1.0, 0.0).astype(BF)
+                return jnp.where(inside, 1.0, 0.0)
 
             for w in range(WIN):
-                lhs[w * CH:(w + 1) * CH, i * 128:(i + 1) * 128] = rm[j, w] * keep(w)
+                lhs[w * CH:(w + 1) * CH, i * 128:(i + 1) * 128] = rm[d, w] * keep(w).astype(BF)
             for t in range(3):
-                upper = jnp.broadcast_to(keep(core * 6 + 2 * t).astype(F32), (8, 128))
-                lower = jnp.broadcast_to(keep(core * 6 + 2 * t + 1).astype(F32), (8, 128))
+                upper = jnp.broadcast_to(keep(core * 6 + 2 * t), (8, 128))
+                lower = jnp.broadcast_to(keep(core * 6 + 2 * t + 1), (8, 128))
                 both = jnp.concatenate([upper, lower], axis=0).astype(BF)
                 lhs[ROWS_MAIN + 16 * t:ROWS_MAIN + 16 * t + 16, i * 128:(i + 1) * 128] = (
-                    rs[j, 16 * t:16 * t + 16, :] * both
+                    rs[d, 16 * t:16 * t + 16, :] * both
                 )
 
-        def column(ct, _):
+        def column(ct, _, begin=begin, size=size):
             col = pl.multiple_of(ct * 256, 256)
-            row = pl.multiple_of(group * 512, 512)
-            acc[:, pl.ds(col, 256)] += jnp.dot(
-                lhs[...], tab[pl.ds(row, 512), pl.ds(col, 256)], preferred_element_type=F32
+            right = jnp.concatenate(
+                [
+                    tab[pl.ds(pl.multiple_of(sender(begin + i) * 128, 128), 128), pl.ds(col, 256)]
+                    for i in range(size)
+                ],
+                axis=0,
             )
+            part = jnp.dot(lhs[:, :size * 128], right, preferred_element_type=F32)
+            if begin:
+                part = part + acc[:, pl.ds(col, 256)]
+            acc[:, pl.ds(col, 256)] = part
             return 0
 
         lax.fori_loop(0, 2 * NF // 256, column, 0)
-        return 0
-
-    lax.fori_loop(0, CHAN // 4, gather_group, 0)
+        begin += size
 
     def sent(d, _):
-        main_copy(d, me).wait_send()
-        src_copy(d, me).wait_send()
+        main_copy(d).wait_send()
+        src_copy(d).wait_send()
         return 0
 
     lax.fori_loop(1, CHAN, sent, 0)
@@ -234,18 +246,19 @@
     masks = slot_masks(8)
 
     def spread(step, _):
-        kb = step // 4
-        c8 = pl.multiple_of(lax.rem(step, 4) * 8, 8)
-        for ri in range(2):
-            col = pl.multiple_of(ri * NF + kb * 128, 128)
-            values = [
-                acc[pl.ds(pl.multiple_of(w * CH + c8, 8), 8), pl.ds(col, 128)] for w in range(WIN)
-            ]
-            for m, out in enumerate(interleave(values, masks)):
-                a_out[kb * 16 + m, ri, pl.ds(c8, 8), :] = out
-        return 0
-
-    lax.fori_loop(0, NKB * 4, spread, 0)
+        kb = step // 2
+        for part in range(2):
+            c8 = pl.multiple_of(lax.rem(step, 2) * 16 + part * 8, 8)
+            for ri in range(2):
+                col = pl.multiple_of(ri * NF + kb * 128, 128)
+                values = [
+                    acc[pl.ds(pl.multiple_of(w * CH + c8, 8), 8), pl.ds(col, 128)] for w in range(WIN)
+                ]
+                for m, out in enumerate(interleave(values, masks)):
+                    a_out[kb * 16 + m, ri, lax.rem(step, 2) * 2 + part] = out
+        return 0
+
+    lax.fori_loop(0, NKB * 2, spread, 0)
 
 
 def spectra(x, wl, sc, tables):
@@ -254,7 +267,7 @@
     return pl.pallas_call(
         spectra_kernel,
         out_shape=(
-            jax.ShapeDtypeStruct((NKB * 16, 2, CH, 128), F32),
+            jax.ShapeDtypeStruct((NKB * 16, 2, CH // 8, 8, 128), F32),
             jax.ShapeDtypeStruct((ROWS_SRC, 2 * NF), BF),
         ),
         in_specs=[
@@ -269,7 +282,7 @@
             pltpu.VMEM((CHAN, WIN, CH, 128), BF),
             pltpu.VMEM((CHAN, ROWS_SRC, 128), BF),
             pltpu.VMEM((W, 2 * NF), BF),
-            pltpu.VMEM((ROWS, 512), BF),
+            pltpu.VMEM((ROWS, 1024), BF),
             pltpu.VMEM((ROWS, 2 * NF), F32),
             pltpu.VMEM((ROWS, NF + 256), BF),
             pltpu.SemaphoreType.DMA((CHAN,)),
@@ -288,6 +301,8 @@
 NC = 3
 CKB = NKB // NC
 CL = CKB * 128
+NQ = 4
+CQ = CH // NQ
 
 
 def cross_kernel(
@@ -404,63 +419,73 @@
     def bins(ch, kbl):
         kb = ch * CKB + kbl
 
-        def spread(q, _):
-            row = pl.multiple_of(q * 8, 8)
+        def spread(qq, _):
+            row = pl.multiple_of(qq * 16, 16)
             for ri in range(2):
                 col = kbl * 128
-                values = []
+                outs = []
+                for q2 in range(2):
+                    q = 2 * qq + q2
+                    values = []
+                    for half in range(2):
+                        for t in range(3):
+                            pair = g_ref[
+                                ch, ri, half, q // 4, lax.rem(q, 4), 16 * t:16 * t + 16, col:col + 128
+                            ].astype(F32)
+                            values += [pair[:8], pair[8:]]
+                    outs.append(interleave(values, masks))
+                for m in range(16):
+                    both = jnp.concatenate([outs[0][m], outs[1][m]], axis=0)
+                    bi[kb * 16 + m, pl.ds(row, 16), ri * 128:ri * 128 + 128] = both.astype(BF)
+            return 0
+
+        lax.fori_loop(0, 8, spread, 0)
+
+    def products(cq):
+        def several(it, _):
+            for p in range(NQ):
+                mp = it * NQ + p
+                results = []
                 for half in range(2):
-                    for t in range(3):
-                        pair = g_ref[
-                            ch, ri, half, q // 4, lax.rem(q, 4), 16 * t:16 * t + 16, col:col + 128
-                        ].astype(F32)
-                        values += [pair[:8], pair[8:]]
-                for m, out in enumerate(interleave(values, masks)):
-                    bi[m, ri, pl.ds(row, 8), :] = out
+                    group = 2 * mp + half
+                    sides = []
+                    for ri in range(2):
+                        tiles = [
+                            jnp.where(
+                                diagonal,
+                                jnp.broadcast_to(
+                                    a_ref[group, ri, cq * (CQ // 8) + c // 8, c % 8:c % 8 + 1, :], (8, 128)
+                                ),
+                                0.0,
+                            )
+                            for c in range(CQ)
+                        ]
+                        sides.append(jnp.concatenate(tiles, axis=0).astype(BF))
+                    left = jnp.concatenate(sides, axis=1)
+                    bre = bi[group, :, 0:128]
+                    bim = bi[group, :, 128:256]
+                    right = jnp.concatenate(
+                        [
+                            jnp.concatenate([bre, bim], axis=1),
+                            jnp.concatenate([-bim, bre], axis=1),
+                        ],
+                        axis=0,
+                    )
+                    results.append(
+                        lax.dot_general(
+                            left, right, (((1,), (1,)), ((), ())), preferred_element_type=F32
+                        )
+                    )
+                row = pl.multiple_of(mp * 16, 16)
+                for ri in range(2):
+                    for c in range(CQ):
+                        both = jnp.concatenate(
+                            [r[c * 8:c * 8 + 8, ri * 128:ri * 128 + 128] for r in results], axis=0
+                        )
+                        xk[pl.ds(pl.multiple_of(ri * NF + row, 16), 16), c * 128:c * 128 + 128] = both.astype(BF)
             return 0
 
-        lax.fori_loop(0, 16, spread, 0)
-
-        def pair_of_groups(mp, _):
-            products = []
-            for half in range(2):
-                m = 2 * mp + half
-                group = kb * 16 + m
-                sides = []
-                for ri in range(2):
-                    tiles = [
-                        jnp.where(
-                            diagonal,
-                            jnp.broadcast_to(a_ref[group, ri, c:c + 1, :], (8, 128)),
-                            0.0,
-                        )
-                        for c in range(CH)
-                    ]
-                    sides.append(jnp.concatenate(tiles, axis=0).astype(BF))
-                left = jnp.concatenate(sides, axis=1)
-                bre, bim = bi[m, 0], bi[m, 1]
-                right = jnp.concatenate(
-                    [
-                        jnp.concatenate([bre, bim], axis=1),
-                        jnp.concatenate([-bim, bre], axis=1),
-                    ],
-                    axis=0,
-                ).astype(BF)
-                products.append(
-                    lax.dot_general(
-                        left, right, (((1,), (1,)), ((), ())), preferred_element_type=F32
-                    )
-                )
-            row = pl.multiple_of(kb * 128 + mp * 16, 16)
-            for ri in range(2):
-                for c in range(CH):
-                    both = jnp.concatenate(
-                        [p[c * 8:c * 8 + 8, ri * 128:ri * 128 + 128] for p in products], axis=0
-                    )
-                    xk[pl.ds(pl.multiple_of(ri * NF + row, 16), 16), c * 128:c * 128 + 128] = both.astype(BF)
-            return 0
-
-        lax.fori_loop(0, 8, pair_of_groups, 0)
+        lax.fori_loop(0, NKB * 8 // NQ, several, 0)
 
     for ch in range(NC):
         step_second(ch)
@@ -480,50 +505,55 @@
         for kbl in range(CKB):
             bins(ch, kbl)
 
-    def exchange(block4, d):
-        c0 = pl.multiple_of(block4 * 4, 4)
+    def exchange(part, d):
+        c0 = pl.multiple_of(part * CQ, CQ)
         return remote(
-            share.at[lax.rem(seg + d, SEG), pl.ds(c0, 4)],
-            landed.at[d - 1, pl.ds(c0, 4)],
-            sx.at[d - 1, block4],
-            rx.at[d - 1, block4],
+            share.at[lax.rem(seg + d, SEG), pl.ds(c0, CQ)],
+            landed.at[d - 1, pl.ds(c0, CQ)],
+            sx.at[d - 1, part],
+            rx.at[d - 1, part],
             segment(d),
         )
 
-    def lags(block4, _):
-        for i2 in range(2):
-            cb = block4 * 2 + i2
+    def quarter(cq, _):
+        products(cq)
+
+        def lags(cb, _):
             col = pl.multiple_of(cb * 256, 256)
             result = jnp.dot(tt[...], xk[:, pl.ds(col, 256)], preferred_element_type=F32)
             for i in range(2):
+                c = cq * CQ + 2 * cb + i
                 flipped = result[:, i * 128:i * 128 + 128].T
                 for g in range(SEG):
                     part = flipped[32 * g:32 * g + 32]
-                    share[g, 2 * cb + i] = part.astype(BF)
+                    share[g, c] = part.astype(BF)
 
                     @pl.when(seg == g)
                     def _():
-                        mine[2 * cb + i] = part
-
+                        mine[c] = part
+
+            return 0
+
+        lax.fori_loop(0, CQ // 2, lags, 0)
         for d in (2, 1, 3):
-            exchange(block4, d).start()
-        return 0
-
-    lax.fori_loop(0, CH // 4, lags, 0)
+            exchange(cq, d).start()
+        return 0
+
+    lax.fori_loop(0, NQ, quarter, 0)
 
     scale = 1.0 / math.sqrt(NF * WIN * SEG)
 
     def finish(block4, _):
         for d in (1, 2, 3):
             exchange(block4, d).wait_recv()
-        c0 = pl.multiple_of(block4 * 4, 4)
-        total = mine[pl.ds(c0, 4)]
+        c0 = pl.multiple_of(block4 * CQ, CQ)
+        total = mine[pl.ds(c0, CQ)]
         for d in (1, 2, 3):
-            total = total + landed[d - 1, pl.ds(c0, 4)].astype(F32)
-        out_ref[pl.ds(c0, 4)] = total * scale
-        return 0
-
-    lax.fori_loop(0, CH // 4, finish, 0)
+            total = total + landed[d - 1, pl.ds(c0, CQ)].astype(F32)
+        out_ref[pl.ds(c0, CQ)] = total * scale
+        return 0
+
+    lax.fori_loop(0, NQ, finish, 0)
 
     for ch in range(NC):
         for ri in halves:
@@ -539,7 +569,7 @@
             exchange(block4, d).wait_send()
         return 0
 
-    lax.fori_loop(0, CH // 4, sent, 0)
+    lax.fori_loop(0, NQ, sent, 0)
 
 
 def cross(a, b, tables):
@@ -553,10 +583,10 @@
         in_specs=[hbm, hbm] + [vmem] * 4,
         out_specs=vmem,
         scratch_shapes=[
-            pltpu.VMEM((NKB * 16, 2, CH, 128), F32),
+            pltpu.VMEM((NKB * 16, 2, CH // 8, 8, 128), F32),
             pltpu.VMEM((NC, 2, 2, 4, 4, ROWS_SRC, CL), BF),
-            pltpu.VMEM((16, 2, VS, 128), F32),
-            pltpu.VMEM((2 * NF, CH * VS), BF),
+            pltpu.VMEM((NKB * 16, VS, 256), BF),
+            pltpu.VMEM((2 * NF, CQ * VS), BF),
             pltpu.VMEM((LAGS, 2 * NF), BF),
             pltpu.VMEM((CH, VS // SEG, LAGS), F32),
             pltpu.VMEM((SEG, CH, VS // SEG, LAGS), BF),
@@ -565,7 +595,7 @@
             dma((NC * 4,)), dma((NC * 4,)),
             dma((NC * 4,)), dma((NC * 4,)),
             dma((NC * 2,)), dma((NC * 2,)),
-            dma((SEG - 1, CH // 4)), dma((SEG - 1, CH // 4)),
+            dma((SEG - 1, NQ)), dma((SEG - 1, NQ)),
             dma((1 + NC * 2,)),
         ],
         compiler_params=pltpu.CompilerParams(

time: 214 us -> 173 us (0.81)
  Pallas kernels: 210 us -> 168 us
    pallas_call x1, Pallas kernels: 96.8 us -> 67.1 us  [spectra(): pl.pallas_call(spectra_kernel, out_shape=(jax.ShapeDtypeStruct((NKB * 16,...]
    pallas_call x1, Pallas kernels: 113 us -> 101 us  [cross(): pl.pallas_call(cross_kernel, out_shape=jax.ShapeDtypeStruct((CH, VS // SE...]
where the time goes in v3:
time: 173 us; the launch traced here: 172 us
  Pallas kernels  168 us (97%)
  local copies, waits for them, and re-layouts  4.57 us (3%)
    pallas_call x1, Pallas kernels, cross(): pl.pallas_call(cross_kernel, out_shape=jax.ShapeDtypeStruct((CH, VS // SE...  101 us
    pallas_call x1, Pallas kernels, spectra(): pl.pallas_call(spectra_kernel, out_shape=(jax.ShapeDtypeStruct((NKB * 16,...  67.1 us

profile of v3, /device:TPU:1, one launch (start us, length us, event | category | flops | bytes accessed | tf_op | source)
XLA Modules:
  0.0 172.4 jit_solution(12613577899818322579)
XLA Ops:
  0.0 1.4 copy.11.sc_ref
  1.4 67.1 %spectra.1 = (f32[144,2,4,8,128]{4,3,2,1,0:T(8,128)}, bf16[48,2304]{1,0:T(8,128)(2,1)}) custom-call(bf16[12,1024,128]{2,1,0:T(8,128)(2,1)} %x_ref.1, s32[12]{0:T(128)} %wl_ref.1, s32[128,1]{1,0:T(8,128)} %copy.11.sc_ref, f32[64,128]{1,0:T(8,128)} %constant.14.clone.ca_ref, f32[64,128]{1,0:T(8,128)} %constant.15.clone.sa_ref, ...), custom_call_target="tpu_custom_call" | custom-call | tf_op jit(solution)/shard_map/spectra/pallas_call | solution.py:267
  68.5 100.7 %cross.1 = f32[32,32,512]{2,1,0:T(8,128)} custom-call(f32[144,2,4,8,128]{4,3,2,1,0:T(8,128)} %get-tuple-element.7.a_hbm, bf16[48,2304]{1,0:T(8,128)(2,1)} %get-tuple-element.8.b_hbm, f32[8,128]{1,0:T(8,128)} %constant.18.clone.la_ref, f32[8,128]{1,0:T(8,128)} %constant.19.clone.ls_ref, f32[64,1152]{1,0:T(8,128)} %constant.16.clone.cb_ref, ...), custom_call_target="tpu_custom_call" | custom-call | tf_op jit(solution)/shard_map/cross/pallas_call | solution.py:580
  169.2 3.2 %copy.13 = f32[32,32,512]{2,1,0:T(8,128)} copy(f32[32,32,512]{2,1,0:T(8,128)} %cross.1) | data formatting | bytes 4194304

commit v4 on v3

--- a/solution.py
+++ b/solution.py
@@ -60,6 +60,35 @@
     return [state[(-m) % 16] for m in range(16)]
 
 
+def whiten(acc, first_row, rows, magp, inv_ref):
+    span = slice(first_row, first_row + rows)
+    magp[:, 0:128] = jnp.zeros((rows, 128), BF)
+    magp[:, NF + 128:NF + 256] = jnp.zeros((rows, 128), BF)
+    for kb in range(NKB):
+        re = acc[span, kb * 128:kb * 128 + 128]
+        im = acc[span, NF + kb * 128:NF + kb * 128 + 128]
+        magp[:, kb * 128 + 128:kb * 128 + 256] = jnp.sqrt(re * re + im * im).astype(BF)
+    band = (
+        jnp.abs(
+            lax.broadcasted_iota(jnp.int32, (384, 128), 0)
+            - 128
+            - lax.broadcasted_iota(jnp.int32, (384, 128), 1)
+        )
+        <= SMOOTH
+    ).astype(F32).astype(BF)
+
+    def scale(kb, _):
+        col = pl.multiple_of(kb * 128, 128)
+        col2 = pl.multiple_of(NF + col, 128)
+        total = jnp.dot(magp[:, pl.ds(col, 384)], band, preferred_element_type=F32)
+        factor = 1.0 / (total * inv_ref[:, pl.ds(col, 128)] + 1e-06)
+        acc[span, pl.ds(col, 128)] = acc[span, pl.ds(col, 128)] * factor
+        acc[span, pl.ds(col2, 128)] = acc[span, pl.ds(col2, 128)] * factor
+        return 0
+
+    lax.fori_loop(0, NKB, scale, 0)
+
+
 def spectra_kernel(
     x_ref, wl_ref, sc_ref, ca_ref, sa_ref, cb_ref, sb_ref, inv_ref,
     a_out, b_out,
@@ -115,9 +144,12 @@
     own.start()
 
     load.wait()
-    hot = (
-        lax.broadcasted_iota(jnp.int32, (VS, CHAN * CH), 1) == sc_ref[...]
-    ).astype(F32).astype(BF)
+    chosen = jnp.broadcast_to(sc_ref[...].astype(F32), (VS, VS)).T
+    channel = lax.broadcasted_iota(jnp.int32, (VS, VS), 1).astype(F32)
+    hot = jnp.concatenate(
+        [(channel + 128.0 * b == chosen).astype(F32).astype(BF) for b in range(CHAN * CH // VS)],
+        axis=1,
+    )
 
     def pick(pair, _):
         first = jnp.dot(hot, xv[2 * pair], preferred_element_type=F32)
@@ -204,6 +236,9 @@
         lax.fori_loop(0, 2 * NF // 256, column, 0)
         begin += size
 
+    out = pltpu.make_async_copy(acc.at[0:ROWS_MAIN], a_out, lsem.at[3])
+    out.start()
+
     def sent(d, _):
         main_copy(d).wait_send()
         src_copy(d).wait_send()
@@ -211,54 +246,9 @@
 
     lax.fori_loop(1, CHAN, sent, 0)
 
-    magp[:, 0:128] = jnp.zeros((ROWS, 128), BF)
-    magp[:, NF + 128:NF + 256] = jnp.zeros((ROWS, 128), BF)
-
-    def magnitude(kb, _):
-        col = pl.multiple_of(kb * 128, 128)
-        re = acc[:, pl.ds(col, 128)]
-        im = acc[:, pl.ds(pl.multiple_of(NF + col, 128), 128)]
-        magp[:, pl.ds(pl.multiple_of(col + 128, 128), 128)] = jnp.sqrt(re * re + im * im).astype(BF)
-        return 0
-
-    lax.fori_loop(0, NKB, magnitude, 0)
-    band = (
-        jnp.abs(
-            lax.broadcasted_iota(jnp.int32, (384, 128), 0)
-            - 128
-            - lax.broadcasted_iota(jnp.int32, (384, 128), 1)
-        )
-        <= SMOOTH
-    ).astype(F32).astype(BF)
-
-    def whiten(kb, _):
-        col = pl.multiple_of(kb * 128, 128)
-        col2 = pl.multiple_of(NF + col, 128)
-        total = jnp.dot(magp[:, pl.ds(col, 384)], band, preferred_element_type=F32)
-        scale = 1.0 / (total * inv_ref[:, pl.ds(col, 128)] + 1e-06)
-        acc[:, pl.ds(col, 128)] = acc[:, pl.ds(col, 128)] * scale
-        acc[:, pl.ds(col2, 128)] = acc[:, pl.ds(col2, 128)] * scale
-        return 0
-
-    lax.fori_loop(0, NKB, whiten, 0)
-
+    whiten(acc, ROWS_MAIN, ROWS_SRC, magp, inv_ref)
     b_out[...] = acc[ROWS_MAIN:, :].astype(BF)
-    masks = slot_masks(8)
-
-    def spread(step, _):
-        kb = step // 2
-        for part in range(2):
-            c8 = pl.multiple_of(lax.rem(step, 2) * 16 + part * 8, 8)
-            for ri in range(2):
-                col = pl.multiple_of(ri * NF + kb * 128, 128)
-                values = [
-                    acc[pl.ds(pl.multiple_of(w * CH + c8, 8), 8), pl.ds(col, 128)] for w in range(WIN)
-                ]
-                for m, out in enumerate(interleave(values, masks)):
-                    a_out[kb * 16 + m, ri, lax.rem(step, 2) * 2 + part] = out
-        return 0
-
-    lax.fori_loop(0, NKB * 2, spread, 0)
+    out.wait()
 
 
 def spectra(x, wl, sc, tables):
@@ -267,7 +257,7 @@
     return pl.pallas_call(
         spectra_kernel,
         out_shape=(
-            jax.ShapeDtypeStruct((NKB * 16, 2, CH // 8, 8, 128), F32),
+            jax.ShapeDtypeStruct((ROWS_MAIN, 2 * NF), F32),
             jax.ShapeDtypeStruct((ROWS_SRC, 2 * NF), BF),
         ),
         in_specs=[
@@ -275,7 +265,7 @@
             pl.BlockSpec(memory_space=pltpu.SMEM),
             vmem, vmem, vmem, vmem, vmem, vmem,
         ],
-        out_specs=(vmem, vmem),
+        out_specs=(pl.BlockSpec(memory_space=pl.ANY), vmem),
         scratch_shapes=[
             pltpu.VMEM((WIN, CHAN * CH, 128), BF),
             pltpu.VMEM((CHAN, ROWS_SRC, 128), BF),
@@ -284,36 +274,38 @@
             pltpu.VMEM((W, 2 * NF), BF),
             pltpu.VMEM((ROWS, 1024), BF),
             pltpu.VMEM((ROWS, 2 * NF), F32),
-            pltpu.VMEM((ROWS, NF + 256), BF),
+            pltpu.VMEM((ROWS_SRC, NF + 256), BF),
             pltpu.SemaphoreType.DMA((CHAN,)),
             pltpu.SemaphoreType.DMA((CHAN,)),
             pltpu.SemaphoreType.DMA((CHAN,)),
             pltpu.SemaphoreType.DMA((CHAN,)),
-            pltpu.SemaphoreType.DMA((3,)),
+            pltpu.SemaphoreType.DMA((4,)),
         ],
         compiler_params=pltpu.CompilerParams(
             collective_id=0, has_side_effects=True, vmem_limit_bytes=60 * 1024 * 1024
         ),
         name="spectra",
-    )(x, wl, sc.reshape(VS, 1), ca, sa, cb, sb, inverse)
+    )(x, wl, sc.reshape(1, VS), ca, sa, cb, sb, inverse)
 
 
 NC = 3
 CKB = NKB // NC
 CL = CKB * 128
-NQ = 4
+NQ = 2
 CQ = CH // NQ
+PC = 4
+PARTS = CH // PC
 
 
 def cross_kernel(
-    a_hbm, b_hbm, la_ref, ls_ref, cb_ref, sb_ref, out_ref,
-    a_ref, g_ref, bi, xk, tt, mine, share, landed,
+    a_hbm, b_hbm, la_ref, ls_ref, cb_ref, sb_ref, inv_ref, out_ref,
+    spec, magp, a_ref, g_ref, bi, xk, tt, share, landed, hop,
     s1, r1, s2, r2, s3, r3, s4, r4, sx, rx, lsem,
 ):
     me = lax.axis_index("chan")
     seg = lax.axis_index("seg")
     z, y, core = me // 8, lax.rem(me // 2, 4), lax.rem(me, 2)
-    load = pltpu.make_async_copy(a_hbm, a_ref, lsem.at[0])
+    load = pltpu.make_async_copy(a_hbm, spec, lsem.at[0])
     load.start()
 
     def at(zz, yy, cc):
@@ -487,73 +479,123 @@
 
         lax.fori_loop(0, NKB * 8 // NQ, several, 0)
 
+    def spread_own(step, _):
+        kb = step // 2
+        for part in range(2):
+            c8 = pl.multiple_of(lax.rem(step, 2) * 16 + part * 8, 8)
+            for ri in range(2):
+                col = pl.multiple_of(ri * NF + kb * 128, 128)
+                values = [
+                    spec[pl.ds(pl.multiple_of(w * CH + c8, 8), 8), pl.ds(col, 128)] for w in range(WIN)
+                ]
+                for m, value in enumerate(interleave(values, masks)):
+                    a_ref[kb * 16 + m, ri, lax.rem(step, 2) * 2 + part] = value
+        return 0
+
     for ch in range(NC):
         step_second(ch)
+    load.wait()
+    whiten(spec, 0, ROWS_MAIN, magp, inv_ref)
     step_third(0)
     step_third(1)
+    lax.fori_loop(0, 6, spread_own, 0)
+    step_third(2)
     step_fourth(0)
-    load.wait()
+    lax.fori_loop(6, 12, spread_own, 0)
+    step_fourth(1)
+    lax.fori_loop(12, NKB * 2, spread_own, 0)
     arrived(0)
     bins(0, 0)
-    step_third(2)
-    step_fourth(1)
+    step_fourth(2)
     bins(0, 1)
-    step_fourth(2)
     bins(0, 2)
     for ch in range(1, NC):
         arrived(ch)
         for kbl in range(CKB):
             bins(ch, kbl)
 
-    def exchange(part, d):
-        c0 = pl.multiple_of(part * CQ, CQ)
+    half = PC // 2
+
+    def chans(part, h):
+        return pl.ds(pl.multiple_of(part * PC + h * half, half), half)
+
+    def outward(part, way):
         return remote(
-            share.at[lax.rem(seg + d, SEG), pl.ds(c0, CQ)],
-            landed.at[d - 1, pl.ds(c0, CQ)],
-            sx.at[d - 1, part],
-            rx.at[d - 1, part],
-            segment(d),
-        )
+            share.at[lax.rem(seg + 2, SEG), chans(part, way)], hop.at[way, part],
+            sx.at[way, part], rx.at[way, part], segment(1 if way == 0 else 3),
+        )
+
+    def direct(part, way):
+        return remote(
+            share.at[lax.rem(seg + (1 if way == 0 else 3), SEG), chans(part, 1 - way)],
+            landed.at[way, chans(part, 1 - way)],
+            sx.at[2 + way, part], rx.at[2 + way, part], segment(1 if way == 0 else 3),
+        )
+
+    def joint(part, way):
+        return remote(
+            share.at[lax.rem(seg + (1 if way == 0 else 3), SEG), chans(part, way)],
+            landed.at[way, chans(part, way)],
+            sx.at[4 + way, part], rx.at[4 + way, part], segment(1 if way == 0 else 3),
+        )
+
+    def pass_on(part):
+        for way in (0, 1):
+            outward(part, way).wait_recv()
+            to = lax.rem(seg + (1 if way == 0 else 3), SEG)
+            total = share[to, chans(part, way)].astype(F32) + hop[way, part].astype(F32)
+            share[to, chans(part, way)] = total.astype(BF)
+            joint(part, way).start()
 
     def quarter(cq, _):
         products(cq)
 
-        def lags(cb, _):
-            col = pl.multiple_of(cb * 256, 256)
-            result = jnp.dot(tt[...], xk[:, pl.ds(col, 256)], preferred_element_type=F32)
-            for i in range(2):
-                c = cq * CQ + 2 * cb + i
-                flipped = result[:, i * 128:i * 128 + 128].T
-                for g in range(SEG):
-                    part = flipped[32 * g:32 * g + 32]
-                    share[g, c] = part.astype(BF)
-
-                    @pl.when(seg == g)
-                    def _():
-                        mine[c] = part
+        def lags(local, _):
+            part = cq * (CQ // PC) + local
+            for pair in range(PC // 2):
+                col = pl.multiple_of(local * PC * VS + pair * 256, 256)
+                result = jnp.dot(tt[...], xk[:, pl.ds(col, 256)], preferred_element_type=F32)
+                for i in range(2):
+                    c = part * PC + 2 * pair + i
+                    flipped = result[:, i * 128:i * 128 + 128].T
+                    for g in range(SEG):
+                        piece = flipped[32 * g:32 * g + 32]
+                        share[g, c] = piece.astype(BF)
+
+                        @pl.when(seg == g)
+                        def _():
+                            out_ref[c] = piece
+
+            for way in (0, 1):
+                outward(part, way).start()
+            for way in (0, 1):
+                direct(part, way).start()
+
+            @pl.when(part > 0)
+            def _():
+                pass_on(part - 1)
 
             return 0
 
-        lax.fori_loop(0, CQ // 2, lags, 0)
-        for d in (2, 1, 3):
-            exchange(cq, d).start()
+        lax.fori_loop(0, CQ // PC, lags, 0)
         return 0
 
     lax.fori_loop(0, NQ, quarter, 0)
 
-    scale = 1.0 / math.sqrt(NF * WIN * SEG)
-
-    def finish(block4, _):
-        for d in (1, 2, 3):
-            exchange(block4, d).wait_recv()
-        c0 = pl.multiple_of(block4 * CQ, CQ)
-        total = mine[pl.ds(c0, CQ)]
-        for d in (1, 2, 3):
-            total = total + landed[d - 1, pl.ds(c0, CQ)].astype(F32)
-        out_ref[pl.ds(c0, CQ)] = total * scale
-        return 0
-
-    lax.fori_loop(0, NQ, finish, 0)
+    pass_on(PARTS - 1)
+
+    def finish(part, _):
+        for way in (0, 1):
+            direct(part, way).wait_recv()
+            joint(part, way).wait_recv()
+        c0 = pl.multiple_of(part * PC, PC)
+        total = out_ref[pl.ds(c0, PC)]
+        for way in (0, 1):
+            total = total + landed[way, pl.ds(c0, PC)].astype(F32)
+        out_ref[pl.ds(c0, PC)] = total
+        return 0
+
+    lax.fori_loop(0, PARTS, finish, 0)
 
     for ch in range(NC):
         for ri in halves:
@@ -564,51 +606,55 @@
                 third(ch, ri, way).wait_send()
             fourth(ch, ri).wait_send()
 
-    def sent(block4, _):
-        for d in (1, 2, 3):
-            exchange(block4, d).wait_send()
-        return 0
-
-    lax.fori_loop(0, NQ, sent, 0)
+    def sent(part, _):
+        for way in (0, 1):
+            outward(part, way).wait_send()
+            direct(part, way).wait_send()
+            joint(part, way).wait_send()
+        return 0
+
+    lax.fori_loop(0, PARTS, sent, 0)
 
 
 def cross(a, b, tables):
-    _, (cb, sb), (la, ls), _ = tables
+    _, (cb, sb), (la, ls), inverse = tables
     vmem = pl.BlockSpec(memory_space=pltpu.VMEM)
     hbm = pl.BlockSpec(memory_space=pl.ANY)
     dma = pltpu.SemaphoreType.DMA
     return pl.pallas_call(
         cross_kernel,
         out_shape=jax.ShapeDtypeStruct((CH, VS // SEG, LAGS), F32),
-        in_specs=[hbm, hbm] + [vmem] * 4,
+        in_specs=[hbm, hbm] + [vmem] * 5,
         out_specs=vmem,
         scratch_shapes=[
+            pltpu.VMEM((ROWS_MAIN, 2 * NF), F32),
+            pltpu.VMEM((ROWS_MAIN, NF + 256), BF),
             pltpu.VMEM((NKB * 16, 2, CH // 8, 8, 128), F32),
             pltpu.VMEM((NC, 2, 2, 4, 4, ROWS_SRC, CL), BF),
             pltpu.VMEM((NKB * 16, VS, 256), BF),
             pltpu.VMEM((2 * NF, CQ * VS), BF),
             pltpu.VMEM((LAGS, 2 * NF), BF),
-            pltpu.VMEM((CH, VS // SEG, LAGS), F32),
             pltpu.VMEM((SEG, CH, VS // SEG, LAGS), BF),
-            pltpu.VMEM((SEG - 1, CH, VS // SEG, LAGS), BF),
+            pltpu.VMEM((2, CH, VS // SEG, LAGS), BF),
+            pltpu.VMEM((2, PARTS, PC // 2, VS // SEG, LAGS), BF),
             dma((NC * 6,)), dma((NC * 6,)),
             dma((NC * 4,)), dma((NC * 4,)),
             dma((NC * 4,)), dma((NC * 4,)),
             dma((NC * 2,)), dma((NC * 2,)),
-            dma((SEG - 1, NQ)), dma((SEG - 1, NQ)),
+            dma((6, PARTS)), dma((6, PARTS)),
             dma((1 + NC * 2,)),
         ],
         compiler_params=pltpu.CompilerParams(
             collective_id=1, has_side_effects=True, vmem_limit_bytes=60 * 1024 * 1024
         ),
         name="cross",
-    )(a, b, la, ls, cb, sb)
+    )(a, b, la, ls, cb, sb, inverse)
 
 
 def on_device(strain_rate, window_length, source_channel):
     tables = jax.tree.map(jnp.asarray, small_tables())
     a, b = spectra(strain_rate, window_length, source_channel, tables)
-    return cross(a, b, tables)
+    return cross(a, b, tables) * (1.0 / math.sqrt(NF * WIN * SEG))
 
 
 def solution(mesh):

time: 173 us -> 166 us (0.960)
  Pallas kernels: 168 us -> 162 us
  local copies, waits for them, and re-layouts: 4.57 us -> 0 us
  other arithmetic: 0 us -> 3.29 us
    pallas_call x1, Pallas kernels: 67.1 us -> 61 us  [spectra(): pl.pallas_call(spectra_kernel, out_shape=(jax.ShapeDtypeStruct((ROWS_MAIN...]
    mul x0 -> x1, other arithmetic: none -> 3.29 us  [on_device(): return cross(a, b, tables) * (1.0 / math.sqrt(NF * WIN * SEG))]
    unnamed x1 -> x0, local copies, waits for them, and re-layouts: 3.19 us -> none
where the time goes in v4:
time: 166 us; the launch traced here: 165 us
  Pallas kernels  162 us (98%)
  other arithmetic  3.29 us (2%)
    pallas_call x1, Pallas kernels, cross(): pl.pallas_call(cross_kernel, out_shape=jax.ShapeDtypeStruct((CH, VS // SE...  101 us
    pallas_call x1, Pallas kernels, spectra(): pl.pallas_call(spectra_kernel, out_shape=(jax.ShapeDtypeStruct((ROWS_MAIN...  61 us

profile of v4, /device:TPU:1, one launch (start us, length us, event | category | flops | bytes accessed | tf_op | source)
XLA Modules:
  0.0 165.4 jit_solution(10280739087734095423)
XLA Ops:
  0.0 61.0 %spectra.1 = (f32[384,2304]{1,0:T(8,128)}, bf16[48,2304]{1,0:T(8,128)(2,1)}) custom-call(bf16[12,1024,128]{2,1,0:T(8,128)(2,1)} %x_ref.1, s32[12]{0:T(128)} %wl_ref.1, s32[1,128]{1,0:T(1,128)} %bitcast.1, f32[64,128]{1,0:T(8,128)} %constant.16.clone.ca_ref, f32[64,128]{1,0:T(8,128)} %constant.17.clone.sa_ref, f32[64,1152]{1,0:T(8,128)} %constant.18.clone.cb_ref, ...), custom_call_target="tpu_custom_call" | custom-call | tf_op jit(solution)/shard_map/spectra/pallas_call | solution.py:257
  61.0 101.0 %cross.1 = f32[32,32,512]{2,1,0:T(8,128)} custom-call(f32[384,2304]{1,0:T(8,128)} %get-tuple-element.7.a_hbm, bf16[48,2304]{1,0:T(8,128)(2,1)} %get-tuple-element.8.b_hbm, f32[8,128]{1,0:T(8,128)} %constant.20.clone.la_ref, f32[8,128]{1,0:T(8,128)} %constant.21.clone.ls_ref, f32[64,1152]{1,0:T(8,128)} %constant.18.clone.cb_ref, ...), custom_call_target="tpu_custom_call" | custom-call | tf_op jit(solution)/shard_map/cross/pallas_call | solution.py:624
  162.1 3.3 %broadcast_multiply_fusion = f32[32,32,512]{2,1,0:T(8,128)} fusion(f32[32,32,512]{2,1,0:T(8,128)} %cross.1), kind=kLoop, calls=%fused_computation | loop fusion | flops 524288 | bytes 4194304 | tf_op jit(solution)/shard_map/mul | solution.py:657

commit v5 on v4

--- a/solution.py
+++ b/solution.py
@@ -294,6 +294,7 @@
 NQ = 2
 CQ = CH // NQ
 PC = 4
+STEP = 8
 PARTS = CH // PC
 
 
@@ -435,8 +436,8 @@
 
     def products(cq):
         def several(it, _):
-            for p in range(NQ):
-                mp = it * NQ + p
+            for p in range(STEP):
+                mp = it * STEP + p
                 results = []
                 for half in range(2):
                     group = 2 * mp + half
@@ -477,7 +478,7 @@
                         xk[pl.ds(pl.multiple_of(ri * NF + row, 16), 16), c * 128:c * 128 + 128] = both.astype(BF)
             return 0
 
-        lax.fori_loop(0, NKB * 8 // NQ, several, 0)
+        lax.fori_loop(0, NKB * 8 // STEP, several, 0)
 
     def spread_own(step, _):
         kb = step // 2

time: 166 us -> 158 us (0.952)
  Pallas kernels: 162 us -> 155 us
    pallas_call x1, Pallas kernels: 101 us -> 93.6 us  [cross(): pl.pallas_call(cross_kernel, out_shape=jax.ShapeDtypeStruct((CH, VS // SE...]
where the time goes in v5:
time: 158 us
  Pallas kernels  155 us (98%)
  other arithmetic  3.29 us (2%)
    pallas_call x1, Pallas kernels, cross(): pl.pallas_call(cross_kernel, out_shape=jax.ShapeDtypeStruct((CH, VS // SE...  93.6 us
    pallas_call x1, Pallas kernels, spectra(): pl.pallas_call(spectra_kernel, out_shape=(jax.ShapeDtypeStruct((ROWS_MAIN...  61 us
    mul x1, other arithmetic, on_device(): return cross(a, b, tables) * (1.0 / math.sqrt(NF * WIN * SEG))  3.29 us

profile of v5, /device:TPU:1, one launch (start us, length us, event | category | flops | bytes accessed | tf_op | source)
XLA Modules:
  0.0 158.0 jit_solution(7325501509141388675)
XLA Ops:
  0.0 61.0 %spectra.1 = (f32[384,2304]{1,0:T(8,128)}, bf16[48,2304]{1,0:T(8,128)(2,1)}) custom-call(bf16[12,1024,128]{2,1,0:T(8,128)(2,1)} %x_ref.1, s32[12]{0:T(128)} %wl_ref.1, s32[1,128]{1,0:T(1,128)} %bitcast.1, f32[64,128]{1,0:T(8,128)} %constant.16.clone.ca_ref, f32[64,128]{1,0:T(8,128)} %constant.17.clone.sa_ref, f32[64,1152]{1,0:T(8,128)} %constant.18.clone.cb_ref, ...), custom_call_target="tpu_custom_call" | custom-call | tf_op jit(solution)/shard_map/spectra/pallas_call | solution.py:257
  61.0 93.6 %cross.1 = f32[32,32,512]{2,1,0:T(8,128)} custom-call(f32[384,2304]{1,0:T(8,128)} %get-tuple-element.7.a_hbm, bf16[48,2304]{1,0:T(8,128)(2,1)} %get-tuple-element.8.b_hbm, f32[8,128]{1,0:T(8,128)} %constant.20.clone.la_ref, f32[8,128]{1,0:T(8,128)} %constant.21.clone.ls_ref, f32[64,1152]{1,0:T(8,128)} %constant.18.clone.cb_ref, ...), custom_call_target="tpu_custom_call" | custom-call | tf_op jit(solution)/shard_map/cross/pallas_call | solution.py:625
  154.7 3.3 %broadcast_multiply_fusion = f32[32,32,512]{2,1,0:T(8,128)} fusion(f32[32,32,512]{2,1,0:T(8,128)} %cross.1), kind=kLoop, calls=%fused_computation | loop fusion | flops 524288 | bytes 4194304 | tf_op jit(solution)/shard_map/mul | solution.py:658
